TPU v7x, 32 devices: a whole 2x2x4 slice. The times are simulated.
32 devices in a mesh: dp: 16 (over z, x, core), tp: 2 (over y).
Axes of the slice: x: 2, y: 2, z: 4, core: 2. Of those that a mesh axis runs over, the one named last changes fastest.
Arguments:
- tokens: bfloat16 [3072, 3584], P('dp', 'tp'), may hold values from -6 to 6
- cotangent: bfloat16 [3072, 3584], P('dp', 'tp'), may hold values from -6 to 6
- working: bfloat16 [16, 2, 3, 2048, 3584], P('dp', 'tp'), may hold values from -0.09375 to 0.09375
- degraded: int32 [16], P('dp'), may hold values from 0 to 1, as said below
- block_map: int32 [16, 16], P('dp'), may hold values from 0 to 1, as said below
- master: float32 [3, 2048, 3584], P(None, ('tp', 'dp')), may hold values from -6 to 6
- moment_one: float32 [3, 2048, 3584], P(None, ('tp', 'dp')), may hold values from -6 to 6
- moment_two: float32 [3, 2048, 3584], P(None, ('tp', 'dp')), may hold values from 0.5 to 8
Outputs:
- input_grad: bfloat16 [3072, 3584], P('dp', 'tp')
- master_next: float32 [3, 2048, 3584], P(None, ('tp', 'dp'))
- moment_one_next: float32 [3, 2048, 3584], P(None, ('tp', 'dp'))
- moment_two_next: float32 [3, 2048, 3584], P(None, ('tp', 'dp'))
Inputs may be any that keep to these rules, and one draw needn't show every extreme that they name: `degraded`: exactly 4 replicas have the value 1. `block_map`: in every row the 16 blocks lie on 1 distinct devices, each of which holds 16 or 16 of them, and at least one holds 16. A row is read only where degraded is 1.
All inputs are finite; a program needn't handle non-finite values.
Results may differ from a plain program's by a relative error of at most 0.0075.
Values may be sent and summed in bfloat16 or wider, within the bound.
No kernel may reach another device: no remote copies, remote signals or barrier semaphores. Data moves between devices by JAX's collectives and lax.ppermute only.
A program may use at most 128 MiB of HBM per device.

v0:
```python
import jax
import jax.numpy as jnp
from jax import lax
from jax.experimental import pallas as pl
from jax.experimental.pallas import tpu as pltpu
from jax.sharding import PartitionSpec as P

BLOCK = 128
BLOCKS = 16


beta_one = 0.9
beta_two = 0.95
learn_rate = 0.05
decay_rate = 0.1
adam_eps = 1e-08
bias_one = 1.0 - 0.9**10
bias_two = 1.0 - 0.95**10


def layout_places(replica_flag, mapping, tp_size, slot_count):
    blocks = jnp.arange(BLOCKS, dtype=jnp.int32)
    canonical = blocks // (BLOCKS // tp_size)
    holder = jnp.where(replica_flag > 0, mapping, canonical)
    earlier = (holder[None, :] == holder[:, None]) & (blocks[None, :] < blocks[:, None])
    slot_rank = jnp.sum(earlier.astype(jnp.int32), axis=1)
    return holder * slot_count + slot_rank


def per_device(tokens, cotangent, working, degraded, block_map, master, moment_one, moment_two):
    tp_size = lax.axis_size("tp")
    replicas = lax.axis_size("dp")
    my_index = lax.axis_index("tp")
    weights = working[0, 0]
    slot_count = weights.shape[1] // BLOCK
    per_dev = BLOCKS // tp_size
    places = layout_places(degraded[0], block_map[0], tp_size, slot_count)
    my_slots = my_index * slot_count + jnp.arange(slot_count, dtype=jnp.int32)
    holding = places[:, None] == my_slots[None, :]
    filled = jnp.any(holding, axis=0).astype(jnp.float32)
    column_mask = jnp.repeat(filled, BLOCK)
    inputs, upstream = (
        lax.all_gather(tokens, "tp", axis=1, tiled=True),
        lax.all_gather(cotangent, "tp", axis=1, tiled=True),
    )
    contract_d = (((1,), (1,)), ((), ()))
    gate_pre = lax.dot_general(inputs, weights[0], contract_d, preferred_element_type=jnp.float32)
    up_pre = lax.dot_general(inputs, weights[1], contract_d, preferred_element_type=jnp.float32)
    hidden_grad = lax.dot_general(
        upstream, weights[2], contract_d, preferred_element_type=jnp.float32
    )
    gate_sig = jax.nn.sigmoid(gate_pre)
    active = gate_pre * gate_sig
    hidden = (active * up_pre * column_mask).astype(jnp.bfloat16)
    gate_grad = (
        hidden_grad * up_pre * gate_sig * (1.0 + gate_pre * (1.0 - gate_sig)) * column_mask
    ).astype(jnp.bfloat16)
    up_grad = (hidden_grad * active * column_mask).astype(jnp.bfloat16)
    partial_value = jnp.dot(gate_grad, weights[0], preferred_element_type=jnp.float32) + jnp.dot(
        up_grad, weights[1], preferred_element_type=jnp.float32
    )
    input_grad = lax.psum_scatter(partial_value, "tp", scatter_dimension=1, tiled=True).astype(
        jnp.bfloat16
    )
    tok_rows = gate_grad.shape[0]
    packed = jnp.stack(
        [
            hidden.reshape(tok_rows, slot_count, BLOCK),
            gate_grad.reshape(tok_rows, slot_count, BLOCK),
            up_grad.reshape(tok_rows, slot_count, BLOCK),
        ],
        axis=2,
    )
    packed = packed.transpose(1, 0, 2, 3).reshape(slot_count, tok_rows, 3 * BLOCK)
    selector = holding.astype(jnp.bfloat16)
    outgoing = jnp.einsum(
        "qs,stc->qtc", selector, packed, preferred_element_type=jnp.float32
    ).astype(jnp.bfloat16)
    incoming = lax.all_to_all(outgoing, "tp", split_axis=0, concat_axis=0, tiled=True)
    owned_acts = jnp.sum(incoming.reshape(tp_size, per_dev, tok_rows, 3 * BLOCK), axis=0)
    owned_kinds = (
        owned_acts.reshape(per_dev, tok_rows, 3, BLOCK)
        .transpose(2, 1, 0, 3)
        .reshape(3, tok_rows, per_dev * BLOCK)
    )
    contract_t = (((0,), (0,)), ((), ()))
    gate_term = lax.dot_general(
        owned_kinds[1], inputs, contract_t, preferred_element_type=jnp.float32
    )
    up_term = lax.dot_general(
        owned_kinds[2], inputs, contract_t, preferred_element_type=jnp.float32
    )
    down_term = lax.dot_general(
        owned_kinds[0], upstream, contract_t, preferred_element_type=jnp.float32
    )
    summed = lax.psum_scatter(
        jnp.stack([gate_term, up_term, down_term], axis=1).astype(jnp.bfloat16),
        "dp",
        scatter_dimension=0,
        tiled=True,
    ).astype(jnp.float32)
    grad_mean = jnp.transpose(summed, (1, 0, 2)) / replicas
    moment_one_next = beta_one * moment_one + (1.0 - beta_one) * grad_mean
    moment_two_next = beta_two * moment_two + (1.0 - beta_two) * grad_mean * grad_mean
    update = (
        moment_one_next / bias_one / (jnp.sqrt(moment_two_next / bias_two) + adam_eps)
        + decay_rate * master
    )
    master_next = master - learn_rate * update
    return (input_grad, master_next, moment_one_next, moment_two_next)


CORES = 2
PAIR = 2
contract_last = (((1,), (1,)), ((), ()))
contract_mid = (((1,), (0,)), ((), ()))


def dot32(a, b, dims):
    return lax.dot_general(a, b, dims, preferred_element_type=jnp.float32)


def weight_specs(kinds, half, sides):
    specs = []
    for kind in kinds:
        for side in sides:
            for j in range(PAIR):

                def where(i, s, kind=kind, side=side, j=j):
                    column = s[2 * s.shape[0] // 3] if side == 0 else 1 - s[2 * s.shape[0] // 3]
                    return (0, 0, kind, s[PAIR * i + j], column)

                specs.append(pl.BlockSpec((1, 1, 1, BLOCK, half), where))
    return specs


def whole_spec(shape):
    return pl.BlockSpec(shape, lambda *_: (0,) * len(shape))


def both(first, second):
    return jnp.concatenate([first[0, 0, 0], second[0, 0, 0]], axis=0)


def own_part(scalars, tokens, cotangent, working):
    pairs = scalars.shape[0] // 6
    rows, half = tokens.shape

    def body(s, t_ref, c_ref, *refs):
        weights, outs = refs[:6], refs[6:]
        i = pl.program_id(0)

        @pl.when(s[2 * pairs + 2 * i] + s[2 * pairs + 2 * i + 1] > 0)
        def _():
            for kind, out in enumerate(outs):
                left = c_ref if kind == 2 else t_ref
                out[0] = dot32(left[...], both(*weights[2 * kind : 2 * kind + 2]), contract_last)

    out = jax.ShapeDtypeStruct((pairs, rows, PAIR * BLOCK), jnp.float32)
    return pl.pallas_call(
        body,
        out_shape=(out,) * 3,
        grid_spec=pltpu.PrefetchScalarGridSpec(
            num_scalar_prefetch=1,
            grid=(pairs,),
            in_specs=[whole_spec(tokens.shape)] * 2 + weight_specs((0, 1, 2), half, (0,)),
            out_specs=(pair_spec(rows),) * 3,
        ),
        cost_estimate=pl.CostEstimate(
            flops=6 * rows * half * pairs * PAIR * BLOCK,
            bytes_accessed=6 * half * pairs * PAIR * BLOCK,
            transcendentals=0,
        ),
        name="own_part",
    )(scalars, tokens, cotangent, *[working] * 6)


def pair_spec(rows):
    return pl.BlockSpec((1, rows, PAIR * BLOCK), lambda i, s: (i, 0, 0))


def act_outputs(pairs, kinds, rows):
    quarter = pairs // 4
    part = (quarter, kinds, rows, BLOCK)

    def theirs_at(i, s):
        at = jnp.minimum(i, 2 * quarter - 1)
        return (at // quarter, 0, at % quarter, 0, 0, 0)

    shapes = (
        jax.ShapeDtypeStruct((2, CORES, *part), jnp.bfloat16),
        jax.ShapeDtypeStruct((CORES, *part), jnp.bfloat16),
        jax.ShapeDtypeStruct((CORES, *part), jnp.bfloat16),
    )
    specs = (
        pl.BlockSpec((1, CORES, 1, kinds, rows, BLOCK), theirs_at),
        pl.BlockSpec(
            (CORES, 1, kinds, rows, BLOCK), lambda i, s: (0, jnp.clip(i - 2 * quarter, 0, quarter - 1), 0, 0, 0)
        ),
        pl.BlockSpec(
            (CORES, 1, kinds, rows, BLOCK), lambda i, s: (0, jnp.clip(i - 3 * quarter, 0, quarter - 1), 0, 0, 0)
        ),
    )
    return shapes, specs


def put_acts(i, pairs, core, values, theirs, far, near):
    quarter = pairs // 4
    narrow = BLOCK // CORES
    pieces = [
        [
            jnp.concatenate(
                [value[:, j * BLOCK + c * narrow : j * BLOCK + (c + 1) * narrow] for j in range(PAIR)], axis=1
            ).astype(jnp.bfloat16)
            for c in range(CORES)
        ]
        for value in values
    ]
    slots = [jnp.bitwise_xor(core, c) for c in range(CORES)]

    @pl.when(i < 2 * quarter)
    def _():
        for kind, piece in enumerate(pieces):
            for c in range(CORES):
                theirs[0, slots[c], 0, kind] = piece[c]

    for ref, low in ((far, 2 * quarter), (near, 3 * quarter)):

        @pl.when((i >= low) & (i < low + quarter))
        def _(ref=ref):
            for kind, piece in enumerate(pieces):
                for c in range(CORES):
                    ref[slots[c], 0, kind] = piece[c]


def gate_up(scalars, other, working, gate, up):
    pairs = scalars.shape[0] // 6
    rows, half = other.shape

    def body(s, other_ref, w0, w1, w2, w3, gate_ref, up_ref, act_ref, slope_ref, *outs):
        i = pl.program_id(0)
        has = [s[2 * pairs + 2 * i + j] for j in range(PAIR)]
        core = s[4 * pairs + 1]

        @pl.when(has[0] + has[1] > 0)
        def _():
            zg = gate_ref[0] + dot32(other_ref[...], both(w0, w1), contract_last)
            zu = up_ref[0] + dot32(other_ref[...], both(w2, w3), contract_last)
            lane = lax.broadcasted_iota(jnp.int32, zg.shape, 1)
            keep = jnp.where(lane < BLOCK, has[0], has[1]) > 0
            sig = jax.nn.sigmoid(zg)
            act = zg * sig
            act_ref[0] = act
            slope_ref[0] = zu * sig * (1.0 + zg * (1.0 - sig))
            put_acts(i, pairs, core, [jnp.where(keep, act * zu, 0.0)], *outs)

        @pl.when(has[0] + has[1] == 0)
        def _():
            put_acts(i, pairs, core, [jnp.zeros((rows, PAIR * BLOCK), jnp.float32)], *outs)

    out = jax.ShapeDtypeStruct((pairs, rows, PAIR * BLOCK), jnp.float32)
    shapes, specs = act_outputs(pairs, 1, rows)
    return pl.pallas_call(
        body,
        out_shape=(out, out, *shapes),
        grid_spec=pltpu.PrefetchScalarGridSpec(
            num_scalar_prefetch=1,
            grid=(pairs,),
            in_specs=[whole_spec(other.shape)] + weight_specs((0, 1), half, (1,)) + [pair_spec(rows)] * 2,
            out_specs=(pair_spec(rows), pair_spec(rows), *specs),
        ),
        cost_estimate=pl.CostEstimate(
            flops=4 * rows * half * pairs * PAIR * BLOCK,
            bytes_accessed=4 * half * pairs * PAIR * BLOCK + 16 * rows * pairs * PAIR * BLOCK,
            transcendentals=rows * pairs * PAIR * BLOCK,
        ),
        name="gate_up",
    )(scalars, other, *[working] * 4, gate, up)


def down_acts(scalars, other, working, partial, act, slope):
    pairs = scalars.shape[0] // 6
    rows, half = other.shape

    def body(s, other_ref, w0, w1, partial_ref, act_ref, slope_ref, grads, *outs):
        i = pl.program_id(0)
        has = [s[2 * pairs + 2 * i + j] for j in range(PAIR)]
        core = s[4 * pairs + 1]

        @pl.when(has[0] + has[1] > 0)
        def _():
            dh = partial_ref[0] + dot32(other_ref[...], both(w0, w1), contract_last)
            lane = lax.broadcasted_iota(jnp.int32, dh.shape, 1)
            keep = jnp.where(lane < BLOCK, has[0], has[1]) > 0
            dgate = jnp.where(keep, dh * slope_ref[0], 0.0)
            dup = jnp.where(keep, dh * act_ref[0], 0.0)
            grads[0, 0] = dgate.astype(jnp.bfloat16)
            grads[0, 1] = dup.astype(jnp.bfloat16)
            put_acts(i, pairs, core, [dgate, dup], *outs)

        @pl.when(has[0] + has[1] == 0)
        def _():
            zero = jnp.zeros((rows, PAIR * BLOCK), jnp.float32)
            grads[...] = jnp.zeros(grads.shape, grads.dtype)
            put_acts(i, pairs, core, [zero, zero], *outs)

    shapes, specs = act_outputs(pairs, 2, rows)
    return pl.pallas_call(
        body,
        out_shape=(jax.ShapeDtypeStruct((pairs, 2, rows, PAIR * BLOCK), jnp.bfloat16), *shapes),
        grid_spec=pltpu.PrefetchScalarGridSpec(
            num_scalar_prefetch=1,
            grid=(pairs,),
            in_specs=[whole_spec(other.shape)] + weight_specs((2,), half, (1,)) + [pair_spec(rows)] * 3,
            out_specs=(pl.BlockSpec((1, 2, rows, PAIR * BLOCK), lambda i, s: (i, 0, 0, 0)), *specs),
        ),
        cost_estimate=pl.CostEstimate(
            flops=2 * rows * half * pairs * PAIR * BLOCK,
            bytes_accessed=2 * half * pairs * PAIR * BLOCK + 20 * rows * pairs * PAIR * BLOCK,
            transcendentals=0,
        ),
        name="down_acts",
    )(scalars, other, *[working] * 2, partial, act, slope)


def input_part(scalars, grads, working, half, side):
    pairs = scalars.shape[0] // 6
    rows = grads.shape[2]

    def body(s, grads_ref, w0, w1, w2, w3, out_ref, total):
        i = pl.program_id(0)

        @pl.when(i == 0)
        def _():
            total[...] = jnp.zeros(total.shape, total.dtype)

        @pl.when(s[2 * pairs + 2 * i] + s[2 * pairs + 2 * i + 1] > 0)
        def _():
            total[...] += dot32(grads_ref[0, 0], both(w0, w1), contract_mid) + dot32(
                grads_ref[0, 1], both(w2, w3), contract_mid
            )

        @pl.when(i == pairs - 1)
        def _():
            out_ref[...] = total[...].astype(out_ref.dtype)

    return pl.pallas_call(
        body,
        out_shape=jax.ShapeDtypeStruct((rows, half), jnp.bfloat16 if side else jnp.float32),
        grid_spec=pltpu.PrefetchScalarGridSpec(
            num_scalar_prefetch=1,
            grid=(pairs,),
            in_specs=[pl.BlockSpec((1, 2, rows, PAIR * BLOCK), lambda i, s: (i, 0, 0, 0))]
            + weight_specs((0, 1), half, (side,)),
            out_specs=whole_spec((rows, half)),
            scratch_shapes=[pltpu.VMEM((rows, half), jnp.float32)],
        ),
        cost_estimate=pl.CostEstimate(
            flops=4 * rows * half * pairs * PAIR * BLOCK,
            bytes_accessed=4 * half * pairs * PAIR * BLOCK,
            transcendentals=0,
        ),
        name="input_other" if side else "input_own",
    )(scalars, grads, *[working] * 4)


def weight_grad(acts, inputs):
    group = len(acts)
    quarter, kinds, rows, _ = acts[0].shape[-4:]
    half = inputs[0].shape[1]
    narrow = BLOCK // CORES
    wide = quarter * BLOCK
    tile = half // 2 if half % (2 * BLOCK) == 0 else half

    def body(*refs):
        a_refs, x_refs = refs[:group], refs[group : 2 * group]
        out_ref, left = refs[2 * group :]

        @pl.when(pl.program_id(0) == 0)
        def _():
            for kind in range(kinds):
                for p in range(quarter):
                    column = jnp.concatenate(
                        [ref[0, p, kind] if len(ref.shape) == 5 else ref[p, kind] for ref in a_refs], axis=0
                    )
                    left[kind, p * BLOCK : (p + 1) * BLOCK, :] = column.T

        right = jnp.concatenate([ref[...] for ref in x_refs], axis=0)
        for kind in range(kinds):
            value = dot32(left[kind], right, contract_mid).astype(jnp.bfloat16)
            for z in range(2 * quarter):
                out_ref[z, kind] = value[z * narrow : (z + 1) * narrow]

    def act_spec(a):
        if a.ndim == 5:
            return pl.BlockSpec((1, *a.shape[1:]), lambda i: (0,) * 5)
        return pl.BlockSpec(a.shape, lambda i: (0,) * 4)

    return pl.pallas_call(
        body,
        out_shape=jax.ShapeDtypeStruct((2 * quarter, kinds, narrow, half), jnp.bfloat16),
        grid=(half // tile,),
        in_specs=[act_spec(a) for a in acts] + [pl.BlockSpec((rows, tile), lambda i: (0, i))] * group,
        out_specs=pl.BlockSpec((2 * quarter, kinds, narrow, tile), lambda i: (0, 0, 0, i)),
        scratch_shapes=[pltpu.VMEM((kinds, wide, group * rows), jnp.bfloat16)],
        cost_estimate=pl.CostEstimate(
            flops=2 * kinds * group * rows * wide * half,
            bytes_accessed=2 * group * rows * half + 2 * kinds * wide * half,
            transcendentals=0,
        ),
    )(*acts, *inputs)


def adam(place, arrived, partial, first, master, moment_one, moment_two, before, replicas):
    _, kinds, rows, half = partial.shape
    step = rows
    state = pl.BlockSpec((1, step, half), lambda k, i, s: (k + first, i, s[1]))

    def body(s, arrived_ref, partial_ref, master_ref, one_ref, two_ref, *refs):
        master_out, one_out, two_out = refs[-3:]
        summed = arrived_ref[0].astype(jnp.float32) + partial_ref[0, 0].astype(jnp.float32)
        grad_mean = summed * (1.0 / replicas)
        one = beta_one * one_ref[0] + (1.0 - beta_one) * grad_mean
        two = beta_two * two_ref[0] + (1.0 - beta_two) * grad_mean * grad_mean
        old = master_ref[0]
        update = one * (1.0 / bias_one) / (jnp.sqrt(two * (1.0 / bias_two)) + adam_eps) + decay_rate * old
        master_out[0] = old - learn_rate * update
        one_out[0] = one
        two_out[0] = two

    aliases = {} if before is None else {6: 0, 7: 1, 8: 2}
    extra = () if before is None else before
    return pl.pallas_call(
        body,
        out_shape=(jax.ShapeDtypeStruct(master.shape, jnp.float32),) * 3,
        grid_spec=pltpu.PrefetchScalarGridSpec(
            num_scalar_prefetch=1,
            grid=(kinds, rows // step),
            in_specs=[
                pl.BlockSpec((1, step, half), lambda k, i, s: (k, i, 0)),
                pl.BlockSpec((1, 1, step, half), lambda k, i, s: (s[0], k, i, 0)),
                state,
                state,
                state,
            ]
            + [pl.BlockSpec(memory_space=pl.ANY)] * len(extra),
            out_specs=(state, state, state),
        ),
        input_output_aliases=aliases,
        cost_estimate=pl.CostEstimate(
            flops=20 * kinds * rows * half, bytes_accessed=28 * kinds * rows * half, transcendentals=0
        ),
        name="adam",
    )(place, arrived, partial, master, moment_one, moment_two, *extra)


def grouped(*args):
    return grouped_step(*args)


def grouped_step(tokens, cotangent, working, degraded, block_map, master, moment_one, moment_two):
    replicas = lax.axis_size("dp")
    tp_size = lax.axis_size("tp")
    inner = 2 * CORES
    depth = replicas // inner
    me = lax.axis_index("tp")
    mine = lax.axis_index("dp")
    z, x, core = mine // inner, (mine // CORES) % 2, mine % CORES
    slot_count = working.shape[3] // BLOCK
    per_dev = BLOCKS // tp_size
    half = tokens.shape[1]

    tp_swap = [(i, (i + 1) % tp_size) for i in range(tp_size)]
    x_swap = [(i, i ^ CORES) for i in range(replicas)]
    core_swap = [(i, i ^ 1) for i in range(replicas)]
    after = lax.optimization_barrier

    def over_y(v):
        return lax.ppermute(v, "tp", tp_swap)

    def over_x(v):
        return lax.ppermute(v, "dp", x_swap)

    def over_core(v):
        return lax.ppermute(v, "dp", core_swap)

    def ring(v, step):
        return lax.ppermute(v, "dp", [(i, (i + step * inner) % replicas) for i in range(replicas)])

    order = jnp.arange(BLOCKS, dtype=jnp.int32)
    along = order % depth
    far_x = 1 - (order // depth) % 2
    far_y = 1 - order // per_dev
    block = ((me + far_y) % tp_size) * per_dev + along * 2 + (x ^ far_x)
    places = layout_places(degraded[0], block_map[0], tp_size, slot_count)
    blocks = jnp.arange(BLOCKS, dtype=jnp.int32)
    place = jnp.sum(jnp.where(block[:, None] == blocks[None, :], places[None, :], 0), axis=1)
    held = place // slot_count == me
    slots = jnp.where(held, place % slot_count, 0)
    extra = jnp.where(blocks == 0, me, jnp.where(blocks == 1, core, 0))
    scalars = jnp.concatenate([slots, held.astype(jnp.int32), extra.astype(jnp.int32)])

    t_own, c_own = tokens, cotangent
    t_other = over_y(t_own)
    c_own_x = over_x(c_own)
    t_own_x = over_x(t_own)
    gate, up, down = own_part(scalars, t_own, c_own, working)
    t_other, c_first = after((t_other, c_own))
    c_other = over_y(c_first)
    c_own_c, t_own_c = over_core(c_own), over_core(t_own)
    act, slope, h_theirs, h_far, h_near = gate_up(scalars, t_other, working, gate, up)
    c_other, h_theirs = after((c_other, h_theirs))
    h_from = over_y(h_theirs)
    c_other_x = over_x(c_other)
    grads, d_theirs, d_far, d_near = down_acts(scalars, c_other, working, down, act, slope)
    h_from, d_theirs = after((h_from, d_theirs))
    d_from = over_y(d_theirs)

    def spread(far, near, came):
        far = far + came[0]
        near_x = over_x(far)
        near = near + came[1]
        return [near, near_x, over_core(near[1]), over_core(near_x[1])]

    hidden_acts = spread(h_far, h_near, h_from)
    c_acts = [
        [c_own, c_own_x, c_own_c, over_core(c_own_x)], [c_other, c_other_x, over_core(c_other), over_core(c_other_x)]
    ]
    hidden_acts[1], t_late = after((hidden_acts[1], t_other))
    t_other_x = over_x(t_late)
    t_acts = [
        [t_own, t_own_x, t_own_c, over_core(t_own_x)], [t_other, t_other_x, over_core(t_other), over_core(t_other_x)]
    ]

    parts = [(2, h, weight_grad(hidden_acts, c_acts[h])) for h in range(2)]
    grad_acts = spread(d_far, d_near, d_from)
    parts += [(0, h, weight_grad(grad_acts, t_acts[h])) for h in range(2)]
    steps = (1, -1)
    moving = [None] * len(parts)
    for low in (0, 2):
        for s in range(1, depth):
            for at in (low, low + 1):
                _, h, partial = parts[at]
                chunk = lax.dynamic_index_in_dim(partial, (z - steps[h] * s) % depth, 0, keepdims=False)
                chunk = chunk if moving[at] is None else chunk + moving[at]
                moving[at] = ring(chunk, steps[h])

    sent = over_y(input_part(scalars, grads, working, half, 1))
    kept = input_part(scalars, grads, working, half, 0)
    input_grad = (kept + sent.astype(jnp.float32)).astype(jnp.bfloat16)

    state = None
    for (first, h, partial), arrived in zip(parts, moving):
        where = jnp.stack([z, (me + h) % tp_size]).astype(jnp.int32)
        state = adam(where, arrived, partial, first, master, moment_one, moment_two, state, replicas)
    return (input_grad, *state)


def solution(mesh):
    replicas, tp_size = mesh.shape["dp"], mesh.shape["tp"]
    inner = 2 * CORES

    def per_part(*args):
        half = args[0].shape[1]
        rows = args[5].shape[1]
        aligned = half % BLOCK == 0 and args[0].shape[0] % 16 == 0 and rows * CORES == BLOCK
        split = replicas % (2 * inner) == 0 and tp_size == 2 and BLOCKS == tp_size * replicas // CORES
        return (grouped if aligned and split else per_device)(*args)

    return jax.shard_map(
        per_part,
        mesh=mesh,
        in_specs=(
            P("dp", "tp"),
            P("dp", "tp"),
            P("dp", "tp", None, None, None),
            P("dp"),
            P("dp", None),
            P(None, ("tp", "dp"), None),
            P(None, ("tp", "dp"), None),
            P(None, ("tp", "dp"), None),
        ),
        out_specs=(
            P("dp", "tp"),
            P(None, ("tp", "dp"), None),
            P(None, ("tp", "dp"), None),
            P(None, ("tp", "dp"), None),
        ),
        check_vma=False,
    )
```

profile of v0, /device:TPU:0, one launch (start us, length us, event | category | flops | bytes accessed | tf_op | source)
XLA Modules:
  0.0 225.1 jit_solution(5026398394060399291)
XLA Ops:
  0.6 3.1 %collective-permute-start = (bf16[192,1792]{1,0:T(8,128)(2,1)}, bf16[192,1792]{1,0:T(8,128)(2,1)S(1)}, u32[]{:S(2)}, u32[]{:S(2)}) collective-permute-start(bf16[192,1792]{1,0:T(8,128)(2,1)} %refs_4_.4), channel_id=1, source_target_pairs={{0,1},{1,0},{2,3},{3,2},{4,5},{5,4},{6,7},{7,6},{8,9},{9,8},{10,11... | collective-permute-start | bytes 2064392 | tf_op jit(solution)/shard_map/ppermute | solution.py:479
  3.7 1.5 collective-permute-start.29
  5.9 0.7 broadcast_select_fusion
  7.0 12.4 %collective-permute-done.other_ref.refs_4_ = bf16[192,1792]{1,0:T(8,128)(2,1)S(1)} collective-permute-done((bf16[192,1792]{1,0:T(8,128)(2,1)}, bf16[192,1792]{1,0:T(8,128)(2,1)S(1)}, u32[]{:S(2)}, u32[]{:S(2)}) %collective-permute-start) | collective-permute-done | bytes 688160 | tf_op jit(solution)/shard_map/ppermute | solution.py:479
  19.3 1.7 collective-permute-start.1
  21.1 0.6 pad_add_fusion.s
  21.7 12.2 %own_part.1 = (f32[8,192,256]{2,1,0:T(8,128)}, f32[8,192,256]{2,1,0:T(8,128)}, f32[8,192,256]{2,1,0:T(8,128)}) custom-call(s32[48]{0:T(128)} %pad_add_fusion.s, bf16[192,1792]{1,0:T(8,128)(2,1)} %refs_4_.4, bf16[192,1792]{1,0:T(8,128)(2,1)} %refs_4_.5, bf16[1,1,3,2048,3584]{4,3,2,1,0:T(8,128)(2,1)} %w3.5, bf16[1,1,3,2048,3584]{4,3,2,1,0:T(8,128)(2,1)} %w3.5, ...), custom_call_target="tpu_custom_call" | custom-call | flops 4227858432 | bytes 22020096 | tf_op jit(solution)/shard_map/own_part/pallas_call | solution.py:160
  33.9 11.6 %gate_up.1 = (f32[8,192,256]{2,1,0:T(8,128)}, f32[8,192,256]{2,1,0:T(8,128)}, bf16[2,2,2,1,192,128]{5,4,3,2,1,0:T(8,128)(2,1)}, bf16[2,2,1,192,128]{4,3,2,1,0:T(8,128)(2,1)}, bf16[2,2,1,192,128]{4,3,2,1,0:T(8,128)(2,1)}) custom-call(s32[48]{0:T(128)} %pad_add_fusion.s, bf16[192,1792]{1,0:T(8,128)(2,1)} %copy-done.5, bf16[1,1,3,2048,3584]{4,3,2,1,0:T(8,128)(2,1)} %w3.5, ...), custom_call_target="tpu_custom_call" | custom-call | flops 2818572288 | bytes 20971520 | tf_op jit(solution)/shard_map/gate_up/pallas_call | solution.py:263
  45.7 4.7 %collective-permute-start.30 = (bf16[192,1792]{1,0:T(8,128)(2,1)S(1)}, bf16[192,1792]{1,0:T(8,128)(2,1)S(1)}, u32[]{:S(2)}, u32[]{:S(2)}) collective-permute-start(bf16[192,1792]{1,0:T(8,128)(2,1)S(1)} %copy-done.7), channel_id=1, source_target_pairs={{0,2},{2,0},{4,6},{6,4},{8,10},{10,8},{12,14},{14,12},{16,18},{18,... | collective-permute-start | bytes 2064392 | tf_op jit(solution)/shard_map/ppermute | solution.py:485
  50.4 0.7 pad_add_fusion.2.s
  51.3 10.1 %down_acts.1 = (bf16[8,2,192,256]{3,2,1,0:T(8,128)(2,1)}, bf16[2,2,2,2,192,128]{5,4,3,2,1,0:T(8,128)(2,1)}, bf16[2,2,2,192,128]{4,3,2,1,0:T(8,128)(2,1)}, bf16[2,2,2,192,128]{4,3,2,1,0:T(8,128)(2,1)}) custom-call(s32[48]{0:T(128)} %pad_add_fusion.s, bf16[192,1792]{1,0:T(8,128)(2,1)} %collective-permute-done.1.other_ref.refs_4_, ...), custom_call_target="tpu_custom_call" | custom-call | flops 1409286144 | bytes 15204352 | tf_op jit(solution)/shard_map/down_acts/pallas_call | solution.py:308
  61.5 1.0 bitcast_add_fusion.8
  62.4 1.0 bitcast_add_fusion.9
  63.5 1.6 collective-permute-start.8
  65.4 6.7 %collective-permute-done.8 = bf16[2,2,1,192,128]{4,3,1,2,0:T(8,128)(2,1)S(1)} collective-permute-done((bf16[2,2,1,192,128]{4,3,1,2,0:T(8,128)(2,1)S(1)}, bf16[2,2,1,192,128]{4,3,1,2,0:T(8,128)(2,1)S(1)}, u32[]{:S(2)}, u32[]{:S(2)}) %collective-permute-start.8) | collective-permute-done | bytes 196640 | tf_op jit(solution)/shard_map/ppermute | solution.py:482
  72.1 0.6 pad_add_fusion.1.s
  72.7 0.5 collective-permute-start.16
  74.4 3.7 %shard_map.114.partial_ref = bf16[4,1,64,1792]{3,2,1,0:T(8,128)(2,1)} custom-call(bf16[2,2,1,192,128]{4,3,2,1,0:T(8,128)(2,1)} %bitcast.66, bf16[2,2,1,192,128]{4,3,2,1,0:T(8,128)(2,1)} %bitcast.68, bf16[2,1,192,128]{3,2,1,0:T(8,128)(2,1)} %bitcast.70, bf16[2,1,192,128]{3,2,1,0:T(8,128)(2,1)} %copy-done.22, bf16[192,1792]{1,0:T(8,128)(2,1)} %refs_4_.5, ...), custom_call_target="tpu_custom_call" | custom-call | flops 704643072 | bytes 3670016 | tf_op jit(solution)/shard_map/pallas_call | solution.py:399
  78.1 1.0 dynamic-slice_bitcast_fusion.2
  79.0 3.4 %collective-permute-start.32 = (bf16[1,64,1792]{2,1,0:T(8,128)(2,1)S(1)}, bf16[1,64,1792]{2,1,0:T(8,128)(2,1)S(1)}, u32[]{:S(2)}, u32[]{:S(2)}) collective-permute-start(bf16[1,64,1792]{2,1,0:T(8,128)(2,1)S(1)} %dynamic-slice_bitcast_fusion.2), channel_id=1, source_target_pairs={{0,8},{2,10},{4,12},{6,14},{8,16},{10,18},{12,20},{14,22},{16,24},... | collective-permute-start | bytes 688136 | tf_op jit(solution)/shard_map/ppermute | solution.py:488
  82.4 9.2 %input_other.1 = bf16[192,1792]{1,0:T(8,128)(2,1)} custom-call(s32[48]{0:T(128)} %pad_add_fusion.s, bf16[8,2,192,256]{3,2,1,0:T(8,128)(2,1)} %get-tuple-element.45.grads_ref, bf16[1,1,3,2048,3584]{4,3,2,1,0:T(8,128)(2,1)} %w3.5, bf16[1,1,3,2048,3584]{4,3,2,1,0:T(8,128)(2,1)} %w3.5, bf16[1,1,3,2048,3584]{4,3,2,1,0:T(8,128)(2,1)} %w3.5, ...), custom_call_target="tpu_custom_call" | custom-call | flops 2818572288 | bytes 14680064 | tf_op jit(solution)/shard_map/input_other/pallas_call | solution.py:347
  91.8 3.5 %collective-permute-start.33 = (bf16[1,64,1792]{2,1,0:T(8,128)(2,1)S(1)}, bf16[1,64,1792]{2,1,0:T(8,128)(2,1)S(1)}, u32[]{:S(2)}, u32[]{:S(2)}) collective-permute-start(bf16[1,64,1792]{2,1,0:T(8,128)(2,1)S(1)} %bitcast_add_fusion.4), channel_id=1, source_target_pairs={{0,8},{2,10},{4,12},{6,14},{8,16},{10,18},{12,20},{14,22},{16,24},... | collective-permute-start | bytes 688136 | tf_op jit(solution)/shard_map/ppermute | solution.py:488
  95.3 9.4 %input_own.1 = f32[192,1792]{1,0:T(8,128)} custom-call(s32[48]{0:T(128)} %pad_add_fusion.s, bf16[8,2,192,256]{3,2,1,0:T(8,128)(2,1)} %get-tuple-element.45.grads_ref, bf16[1,1,3,2048,3584]{4,3,2,1,0:T(8,128)(2,1)} %w3.5, bf16[1,1,3,2048,3584]{4,3,2,1,0:T(8,128)(2,1)} %w3.5, bf16[1,1,3,2048,3584]{4,3,2,1,0:T(8,128)(2,1)} %w3.5, bf16[1,1,3,2048,3584]{4,3,2,1,0:T(8,128)(2,1)} %w3.5), custom_call_target="tpu_custom_call" | custom-call | flops 2818572288 | bytes 14680064 | tf_op jit(solution)/shard_map/input_own/pallas_call | solution.py:347
  104.7 0.5 collective-permute-start.25
  105.2 0.7 bitcast_add_fusion.5
  105.9 5.8 %collective-permute-done.4 = bf16[2,2,2,2,192,128]{5,4,3,2,1,0:T(8,128)(2,1)} collective-permute-done((bf16[2,2,2,2,192,128]{5,4,3,2,1,0:T(8,128)(2,1)}, bf16[2,2,2,2,192,128]{5,4,3,2,1,0:T(8,128)(2,1)}, u32[]{:S(2)}, u32[]{:S(2)}) %collective-permute-start.4) | collective-permute-done | bytes 786464 | tf_op jit(solution)/shard_map/ppermute | solution.py:479
  111.7 1.3 fusion
  113.0 1.1 collective-permute-start.5
  114.2 1.0 collective-permute-start.9
  115.2 0.9 copy-done.17
  116.1 3.7 %shard_map.113.partial_ref = bf16[4,1,64,1792]{3,2,1,0:T(8,128)(2,1)} custom-call(bf16[2,2,1,192,128]{4,3,2,1,0:T(8,128)(2,1)} %bitcast.67, bf16[2,2,1,192,128]{4,3,2,1,0:T(8,128)(2,1)} %bitcast.69, bf16[2,1,192,128]{3,2,1,0:T(8,128)(2,1)} %bitcast.71, bf16[2,1,192,128]{3,2,1,0:T(8,128)(2,1)} %copy-done.22, ...), custom_call_target="tpu_custom_call" | custom-call | flops 704643072 | bytes 3670016 | tf_op jit(solution)/shard_map/pallas_call | solution.py:399
  119.8 1.0 dynamic-slice_bitcast_fusion.3
  120.8 4.3 %collective-permute-done.5.refs_1_ = bf16[2,2,2,192,128]{4,3,2,1,0:T(8,128)(2,1)S(1)} collective-permute-done((bf16[2,2,2,192,128]{4,3,2,1,0:T(8,128)(2,1)S(1)}, bf16[2,2,2,192,128]{4,3,2,1,0:T(8,128)(2,1)S(1)}, u32[]{:S(2)}, u32[]{:S(2)}) %collective-permute-start.5) | collective-permute-done | bytes 393248 | tf_op jit(solution)/shard_map/ppermute | solution.py:482
  125.1 3.1 %collective-permute-start.26 = (bf16[1,64,1792]{2,1,0:T(8,128)(2,1)S(1)}, bf16[1,64,1792]{2,1,0:T(8,128)(2,1)S(1)}, u32[]{:S(2)}, u32[]{:S(2)}) collective-permute-start(bf16[1,64,1792]{2,1,0:T(8,128)(2,1)S(1)} %dynamic-slice_bitcast_fusion.3), channel_id=1, source_target_pairs={{0,24},{2,26},{4,28},{6,30},{8,0},{10,2},{12,4},{14,6},{16,8},{18,... | collective-permute-start | bytes 688136 | tf_op jit(solution)/shard_map/ppermute | solution.py:488
  128.2 3.5 %collective-permute-done.26 = bf16[1,64,1792]{2,1,0:T(8,128)(2,1)S(1)} collective-permute-done((bf16[1,64,1792]{2,1,0:T(8,128)(2,1)S(1)}, bf16[1,64,1792]{2,1,0:T(8,128)(2,1)S(1)}, u32[]{:S(2)}, u32[]{:S(2)}) %collective-permute-start.26) | collective-permute-done | bytes 229408 | tf_op jit(solution)/shard_map/ppermute | solution.py:488
  131.7 1.0 bitcast_add_fusion.6
  132.7 0.6 collective-permute-start.10
  133.3 0.4 collective-permute-start.2
  133.7 4.7 %collective-permute-done.9.refs_5_ = bf16[192,1792]{1,0:T(8,128)(2,1)} collective-permute-done((bf16[192,1792]{1,0:T(8,128)(2,1)S(1)}, bf16[192,1792]{1,0:T(8,128)(2,1)}, u32[]{:S(2)}, u32[]{:S(2)}) %collective-permute-start.9) | collective-permute-done | bytes 688160 | tf_op jit(solution)/shard_map/ppermute | solution.py:482
  138.4 1.1 collective-permute-start.34
  139.6 2.7 %collective-permute-start.27 = (bf16[1,64,1792]{2,1,0:T(8,128)(2,1)S(1)}, bf16[1,64,1792]{2,1,0:T(8,128)(2,1)S(1)}, u32[]{:S(2)}, u32[]{:S(2)}) collective-permute-start(bf16[1,64,1792]{2,1,0:T(8,128)(2,1)S(1)} %bitcast_add_fusion.6), channel_id=1, source_target_pairs={{0,24},{2,26},{4,28},{6,30},{8,0},{10,2},{12,4},{14,6},{16,8},{18,... | collective-permute-start | bytes 688136 | tf_op jit(solution)/shard_map/ppermute | solution.py:488
  142.4 4.9 %shard_map.112.partial_ref = bf16[4,2,64,1792]{3,2,1,0:T(8,128)(2,1)} custom-call(bf16[2,2,2,192,128]{4,3,2,1,0:T(8,128)(2,1)} %copy-done.4, bf16[2,2,2,192,128]{4,3,2,1,0:T(8,128)(2,1)} %copy-done.9, bf16[2,2,192,128]{3,2,1,0:T(8,128)(2,1)} %copy-done.12, bf16[2,2,192,128]{3,2,1,0:T(8,128)(2,1)} %copy-done.13, bf16[192,1792]{1,0:T(8,128)(2,1)} %refs_4_.4, ...), custom_call_target="tpu_custom_call" | custom-call | flops 1409286144 | bytes 4587520 | tf_op jit(solution)/shard_map/pallas_call | solution.py:399
  147.3 1.0 dynamic-slice_bitcast_fusion
  148.3 3.2 %collective-permute-done.27 = bf16[1,64,1792]{2,1,0:T(8,128)(2,1)S(1)} collective-permute-done((bf16[1,64,1792]{2,1,0:T(8,128)(2,1)S(1)}, bf16[1,64,1792]{2,1,0:T(8,128)(2,1)S(1)}, u32[]{:S(2)}, u32[]{:S(2)}) %collective-permute-start.27) | collective-permute-done | bytes 229408 | tf_op jit(solution)/shard_map/ppermute | solution.py:488
  151.5 0.6 collective-permute-start.18
  152.1 1.6 bitcast_add_fusion.7
  153.7 3.2 %collective-permute-start.28 = (bf16[1,64,1792]{2,1,0:T(8,128)(2,1)}, bf16[1,64,1792]{2,1,0:T(8,128)(2,1)}, u32[]{:S(2)}, u32[]{:S(2)}) collective-permute-start(bf16[1,64,1792]{2,1,0:T(8,128)(2,1)} %bitcast_add_fusion.7), channel_id=1, source_target_pairs={{0,24},{2,26},{4,28},{6,30},{8,0},{10,2},{12,4},{14,6},{16,8},{18,... | collective-permute-start | bytes 688136 | tf_op jit(solution)/shard_map/ppermute | solution.py:488
  157.0 4.9 %shard_map.111.partial_ref = bf16[4,2,64,1792]{3,2,1,0:T(8,128)(2,1)} custom-call(bf16[2,2,2,192,128]{4,3,2,1,0:T(8,128)(2,1)} %copy-done.4, bf16[2,2,2,192,128]{4,3,2,1,0:T(8,128)(2,1)} %copy-done.9, bf16[2,2,192,128]{3,2,1,0:T(8,128)(2,1)} %copy-done.12, bf16[2,2,192,128]{3,2,1,0:T(8,128)(2,1)} %copy-done.13, bf16[192,1792]{1,0:T(8,128)(2,1)} %copy-done.5, ...), custom_call_target="tpu_custom_call" | custom-call | flops 1409286144 | bytes 4587520 | tf_op jit(solution)/shard_map/pallas_call | solution.py:399
  161.9 1.2 dynamic-slice_bitcast_fusion.1
  163.3 3.6 %collective-permute-done.18 = bf16[2,64,1792]{2,1,0:T(8,128)(2,1)} collective-permute-done((bf16[2,64,1792]{2,1,0:T(8,128)(2,1)S(1)}, bf16[2,64,1792]{2,1,0:T(8,128)(2,1)}, u32[]{:S(2)}, u32[]{:S(2)}) %collective-permute-start.18) | collective-permute-done | bytes 458784 | tf_op jit(solution)/shard_map/ppermute | solution.py:488
  166.9 1.1 bitcast_add_fusion
  168.0 13.5 %collective-permute-done.12 = bf16[2,64,1792]{2,1,0:T(8,128)(2,1)S(1)} collective-permute-done((bf16[2,64,1792]{2,1,0:T(8,128)(2,1)S(1)}, bf16[2,64,1792]{2,1,0:T(8,128)(2,1)S(1)}, u32[]{:S(2)}, u32[]{:S(2)}) %collective-permute-start.12) | collective-permute-done | bytes 458784 | tf_op jit(solution)/shard_map/ppermute | solution.py:488
  181.6 0.6 collective-permute-start.13
  182.2 9.2 %collective-permute-done.19 = bf16[2,64,1792]{2,1,0:T(8,128)(2,1)S(1)} collective-permute-done((bf16[2,64,1792]{2,1,0:T(8,128)(2,1)S(1)}, bf16[2,64,1792]{2,1,0:T(8,128)(2,1)S(1)}, u32[]{:S(2)}, u32[]{:S(2)}) %collective-permute-start.19) | collective-permute-done | bytes 458784 | tf_op jit(solution)/shard_map/ppermute | solution.py:488
  191.5 9.7 %collective-permute-done.13 = bf16[2,64,1792]{2,1,0:T(8,128)(2,1)S(1)} collective-permute-done((bf16[2,64,1792]{2,1,0:T(8,128)(2,1)S(1)}, bf16[2,64,1792]{2,1,0:T(8,128)(2,1)S(1)}, u32[]{:S(2)}, u32[]{:S(2)}) %collective-permute-start.13) | collective-permute-done | bytes 458784 | tf_op jit(solution)/shard_map/ppermute | solution.py:488
  201.3 0.8 collective-permute-start.14
  202.1 2.1 add_convert_fusion
  204.1 3.6 %adam.4 = (f32[3,64,3584]{2,1,0:T(8,128)}, f32[3,64,3584]{2,1,0:T(8,128)}, f32[3,64,3584]{2,1,0:T(8,128)}) custom-call(s32[2]{0:T(128)} %pad_add_fusion.2.s, bf16[1,64,1792]{2,1,0:T(8,128)(2,1)} %collective-permute-done.34.arrived_ref, bf16[4,1,64,1792]{3,2,1,0:T(8,128)(2,1)} %shard_map.114.partial_ref, f32[3,64,3584]{2,1,0:T(8,128)} %master_ref.7, ...), custom_call_target="tpu_custom_call" | custom-call | flops 2293760 | bytes 3211264 | tf_op jit(solution)/shard_map/adam/pallas_call | solution.py:433
  207.8 3.6 %adam.5 = (f32[3,64,3584]{2,1,0:T(8,128)}, f32[3,64,3584]{2,1,0:T(8,128)}, f32[3,64,3584]{2,1,0:T(8,128)}) custom-call(s32[2]{0:T(128)} %pad_add_fusion.1.s, bf16[1,64,1792]{2,1,0:T(8,128)(2,1)} %collective-permute-done.28.arrived_ref, bf16[4,1,64,1792]{3,2,1,0:T(8,128)(2,1)} %shard_map.113.partial_ref, ...), custom_call_target="tpu_custom_call", output_to_operand_aliasing={{0}: (6, {}), {1}: (7, {}), {2}: (8, {})} | custom-call | flops 2293760 | bytes 3211264 | tf_op jit(solution)/shard_map/adam/pallas_call | solution.py:433
  211.4 0.8 copy-done.19
  212.2 4.2 %adam.6 = (f32[3,64,3584]{2,1,0:T(8,128)}, f32[3,64,3584]{2,1,0:T(8,128)}, f32[3,64,3584]{2,1,0:T(8,128)}) custom-call(s32[2]{0:T(128)} %pad_add_fusion.2.s, bf16[2,64,1792]{2,1,0:T(8,128)(2,1)} %copy-done.19, bf16[4,2,64,1792]{3,2,1,0:T(8,128)(2,1)} %shard_map.112.partial_ref, ...), custom_call_target="tpu_custom_call", output_to_operand_aliasing={{0}: (6, {}), {1}: (7, {}), {2}: (8, {})} | custom-call | flops 4587520 | bytes 6422528 | tf_op jit(solution)/shard_map/adam/pallas_call | solution.py:433
  216.4 3.6 %collective-permute-done.14.arrived_ref = bf16[2,64,1792]{2,1,0:T(8,128)(2,1)S(1)} collective-permute-done((bf16[2,64,1792]{2,1,0:T(8,128)(2,1)S(1)}, bf16[2,64,1792]{2,1,0:T(8,128)(2,1)S(1)}, u32[]{:S(2)}, u32[]{:S(2)}) %collective-permute-start.14) | collective-permute-done | bytes 458784 | tf_op jit(solution)/shard_map/ppermute | solution.py:488
  220.0 0.8 copy-done.18
  220.8 4.2 %adam.7 = (f32[3,64,3584]{2,1,0:T(8,128)}, f32[3,64,3584]{2,1,0:T(8,128)}, f32[3,64,3584]{2,1,0:T(8,128)}) custom-call(s32[2]{0:T(128)} %pad_add_fusion.1.s, bf16[2,64,1792]{2,1,0:T(8,128)(2,1)} %copy-done.18, bf16[4,2,64,1792]{3,2,1,0:T(8,128)(2,1)} %shard_map.111.partial_ref, ...), custom_call_target="tpu_custom_call", output_to_operand_aliasing={{0}: (6, {}), {1}: (7, {}), {2}: (8, {})} | custom-call | flops 4587520 | bytes 6422528 | tf_op jit(solution)/shard_map/adam/pallas_call | solution.py:433
  (100 shorter events, 3.2 us)
Async XLA Ops:
  0.6 18.7 %collective-permute-start = (bf16[192,1792]{1,0:T(8,128)(2,1)}, bf16[192,1792]{1,0:T(8,128)(2,1)S(1)}, u32[]{:S(2)}, u32[]{:S(2)}) collective-permute-start(bf16[192,1792]{1,0:T(8,128)(2,1)} %refs_4_.4), channel_id=1, source_target_pairs={{0,1},{1,0},{2,3},{3,2},{4,5},{5,4},{6,7},{7,6},{8,9},{9,8},{10,11... | collective-permute-start | bytes 2064392 | tf_op jit(solution)/shard_map/ppermute | solution.py:479
  3.7 47.4 %collective-permute-start.29 = (bf16[192,1792]{1,0:T(8,128)(2,1)}, bf16[192,1792]{1,0:T(8,128)(2,1)}, u32[]{:S(2)}, u32[]{:S(2)}) collective-permute-start(bf16[192,1792]{1,0:T(8,128)(2,1)} %refs_4_.5), channel_id=1, source_target_pairs={{0,4},{2,6},{4,0},{6,2},{8,12},{10,14},{12,8},{14,10},{16,20},{18,... | collective-permute-start | bytes 2064392 | tf_op jit(solution)/shard_map/ppermute | solution.py:482
  19.3 14.5 %copy-start.5 = (bf16[192,1792]{1,0:T(8,128)(2,1)}, bf16[192,1792]{1,0:T(8,128)(2,1)S(1)}, u32[]{:S(2)}) copy-start(bf16[192,1792]{1,0:T(8,128)(2,1)S(1)} %collective-permute-done.other_ref.refs_4_) | copy-start | bytes 2064388
  19.3 26.1 %collective-permute-start.1 = (bf16[192,1792]{1,0:T(8,128)(2,1)}, bf16[192,1792]{1,0:T(8,128)(2,1)}, u32[]{:S(2)}, u32[]{:S(2)}) collective-permute-start(bf16[192,1792]{1,0:T(8,128)(2,1)} %refs_4_.5), channel_id=1, source_target_pairs={{0,1},{1,0},{2,3},{3,2},{4,5},{5,4},{6,7},{7,6},{8,9},{9,8},{10,11... | collective-permute-start | bytes 2064392 | tf_op jit(solution)/shard_map/ppermute | solution.py:479
  33.8 11.8 %copy-start.7 = (bf16[192,1792]{1,0:T(8,128)(2,1)S(1)}, bf16[192,1792]{1,0:T(8,128)(2,1)}, u32[]{:S(2)}) copy-start(bf16[192,1792]{1,0:T(8,128)(2,1)} %refs_4_.5) | copy-start | bytes 2064388
  33.9 16.6 %copy-start.8 = (bf16[192,1792]{1,0:T(8,128)(2,1)S(1)}, bf16[192,1792]{1,0:T(8,128)(2,1)}, u32[]{:S(2)}) copy-start(bf16[192,1792]{1,0:T(8,128)(2,1)} %refs_4_.4) | copy-start | bytes 2064388
  45.5 16.0 %collective-permute-start.3 = (bf16[2,2,2,1,192,128]{5,4,2,1,3,0:T(8,128)(2,1)}, bf16[2,2,2,1,192,128]{5,4,2,1,3,0:T(8,128)(2,1)}, u32[]{:S(2)}, u32[]{:S(2)}) collective-permute-start(bf16[2,2,2,1,192,128]{5,4,2,1,3,0:T(8,128)(2,1)} %bitcast.72), channel_id=1, source_target_pairs={{0,1},{1,0},{2,3},{3,2},{4,5},{5,4},{6,7},{7,6},{8,9},{9,8},{10,11... | collective-permute-start | bytes 1179656 | tf_op jit(solution)/shard_map/ppermute | solution.py:479
  45.7 27.1 %collective-permute-start.30 = (bf16[192,1792]{1,0:T(8,128)(2,1)S(1)}, bf16[192,1792]{1,0:T(8,128)(2,1)S(1)}, u32[]{:S(2)}, u32[]{:S(2)}) collective-permute-start(bf16[192,1792]{1,0:T(8,128)(2,1)S(1)} %copy-done.7), channel_id=1, source_target_pairs={{0,2},{2,0},{4,6},{6,4},{8,10},{10,8},{12,14},{14,12},{16,18},{18,... | collective-permute-start | bytes 2064392 | tf_op jit(solution)/shard_map/ppermute | solution.py:485
  50.4 22.8 %collective-permute-start.15 = (bf16[192,1792]{1,0:T(8,128)(2,1)S(1)}, bf16[192,1792]{1,0:T(8,128)(2,1)}, u32[]{:S(2)}, u32[]{:S(2)}) collective-permute-start(bf16[192,1792]{1,0:T(8,128)(2,1)S(1)} %copy-done.8), channel_id=1, source_target_pairs={{0,4},{2,6},{4,0},{6,2},{8,12},{10,14},{12,8},{14,10},{16,20},{18,... | collective-permute-start | bytes 2064392 | tf_op jit(solution)/shard_map/ppermute | solution.py:482
  51.1 22.2 %collective-permute-start.31 = (bf16[192,1792]{1,0:T(8,128)(2,1)}, bf16[192,1792]{1,0:T(8,128)(2,1)S(1)}, u32[]{:S(2)}, u32[]{:S(2)}) collective-permute-start(bf16[192,1792]{1,0:T(8,128)(2,1)} %collective-permute-done.29.refs_5_), channel_id=1, source_target_pairs={{0,2},{2,0},{4,6},{6,4},{8,10},{10,8},{12,14},{14,12},{16,18},{18,... | collective-permute-start | bytes 2064392 | tf_op jit(solution)/shard_map/ppermute | solution.py:485
  51.3 10.1 %copy-start.24 = (bf16[2,2,1,192,128]{4,3,2,1,0:T(8,128)(2,1)S(1)}, bf16[2,2,1,192,128]{4,3,2,1,0:T(8,128)(2,1)}, u32[]{:S(2)}) copy-start(bf16[2,2,1,192,128]{4,3,2,1,0:T(8,128)(2,1)} %get-tuple-element.54) | copy-start | bytes 589828
  51.3 11.1 %copy-start.23 = (bf16[2,2,1,192,128]{4,3,2,1,0:T(8,128)(2,1)S(1)}, bf16[2,2,1,192,128]{4,3,2,1,0:T(8,128)(2,1)}, u32[]{:S(2)}) copy-start(bf16[2,2,1,192,128]{4,3,2,1,0:T(8,128)(2,1)} %get-tuple-element.51) | copy-start | bytes 589828
  62.4 11.3 %copy-start.10 = (bf16[2,2,1,192,128]{4,3,1,0,2:T(8,128)(2,1)}, bf16[2,2,1,192,128]{4,3,1,0,2:T(8,128)(2,1)S(1)}, u32[]{:S(2)}) copy-start(bf16[2,2,1,192,128]{4,3,1,0,2:T(8,128)(2,1)S(1)} %bitcast_add_fusion.8) | copy-start | bytes 589828
  63.5 8.6 %collective-permute-start.8 = (bf16[2,2,1,192,128]{4,3,1,2,0:T(8,128)(2,1)S(1)}, bf16[2,2,1,192,128]{4,3,1,2,0:T(8,128)(2,1)S(1)}, u32[]{:S(2)}, u32[]{:S(2)}) collective-permute-start(bf16[2,2,1,192,128]{4,3,1,2,0:T(8,128)(2,1)S(1)} %bitcast_add_fusion.9), channel_id=1, source_target_pairs={{0,4},{2,6},{4,0},{6,2},{8,12},{10,14},{12,8},{14,10},{16,20},{18,... | collective-permute-start | bytes 589832 | tf_op jit(solution)/shard_map/ppermute | solution.py:482
  65.1 8.6 %collective-permute-start.21 = (bf16[2,1,192,128]{3,2,0,1:T(8,128)(2,1)S(1)}, bf16[2,1,192,128]{3,2,0,1:T(8,128)(2,1)S(1)}, u32[]{:S(2)}, u32[]{:S(2)}) collective-permute-start(bf16[2,1,192,128]{3,2,0,1:T(8,128)(2,1)S(1)} %slice_bitcast_fusion.5), channel_id=1, source_target_pairs={{0,2},{2,0},{4,6},{6,4},{8,10},{10,8},{12,14},{14,12},{16,18},{18,... | collective-permute-start | bytes 294920 | tf_op jit(solution)/shard_map/ppermute | solution.py:485
  72.0 1.7 copy-start.11
  72.0 1.6 collective-permute-start.22
  72.7 1.0 copy-start.14
  72.7 60.0 %collective-permute-start.16 = (bf16[192,1792]{1,0:T(8,128)(2,1)S(1)}, bf16[192,1792]{1,0:T(8,128)(2,1)}, u32[]{:S(2)}, u32[]{:S(2)}) collective-permute-start(bf16[192,1792]{1,0:T(8,128)(2,1)S(1)} %copy-done.8), channel_id=1, source_target_pairs={{0,2},{2,0},{4,6},{6,4},{8,10},{10,8},{12,14},{14,12},{16,18},{18,... | collective-permute-start | bytes 2064392 | tf_op jit(solution)/shard_map/ppermute | solution.py:485
  73.2 60.0 %collective-permute-start.17 = (bf16[192,1792]{1,0:T(8,128)(2,1)}, bf16[192,1792]{1,0:T(8,128)(2,1)}, u32[]{:S(2)}, u32[]{:S(2)}) collective-permute-start(bf16[192,1792]{1,0:T(8,128)(2,1)} %collective-permute-done.15.refs_5_), channel_id=1, source_target_pairs={{0,2},{2,0},{4,6},{6,4},{8,10},{10,8},{12,14},{14,12},{16,18},{18,... | collective-permute-start | bytes 2064392 | tf_op jit(solution)/shard_map/ppermute | solution.py:485
  73.3 0.8 copy-start.15
  73.3 31.3 %collective-permute-start.23 = (bf16[192,1792]{1,0:T(8,128)(2,1)}, bf16[192,1792]{1,0:T(8,128)(2,1)}, u32[]{:S(2)}, u32[]{:S(2)}) collective-permute-start(bf16[192,1792]{1,0:T(8,128)(2,1)} %collective-permute-done.1.other_ref.refs_4_), channel_id=1, source_target_pairs={{0,4},{2,6},{4,0},{6,2},{8,12},{10,14},{12,8},{14,10},{16,20},{18,... | collective-permute-start | bytes 2064392 | tf_op jit(solution)/shard_map/ppermute | solution.py:482
  73.7 0.6 copy-start.21
  73.7 0.7 copy-start.22
  79.0 12.7 %collective-permute-start.32 = (bf16[1,64,1792]{2,1,0:T(8,128)(2,1)S(1)}, bf16[1,64,1792]{2,1,0:T(8,128)(2,1)S(1)}, u32[]{:S(2)}, u32[]{:S(2)}) collective-permute-start(bf16[1,64,1792]{2,1,0:T(8,128)(2,1)S(1)} %dynamic-slice_bitcast_fusion.2), channel_id=1, source_target_pairs={{0,8},{2,10},{4,12},{6,14},{8,16},{10,18},{12,20},{14,22},{16,24},... | collective-permute-start | bytes 688136 | tf_op jit(solution)/shard_map/ppermute | solution.py:488
  82.4 9.3 %copy-start.2 = (bf16[4,1,64,1792]{3,2,1,0:T(8,128)(2,1)S(1)}, bf16[4,1,64,1792]{3,2,1,0:T(8,128)(2,1)}, u32[]{:S(2)}) copy-start(bf16[4,1,64,1792]{3,2,1,0:T(8,128)(2,1)} %shard_map.114.partial_ref) | copy-start | bytes 2752516
  91.6 20.1 %collective-permute-start.4 = (bf16[2,2,2,2,192,128]{5,4,3,2,1,0:T(8,128)(2,1)}, bf16[2,2,2,2,192,128]{5,4,3,2,1,0:T(8,128)(2,1)}, u32[]{:S(2)}, u32[]{:S(2)}) collective-permute-start(bf16[2,2,2,2,192,128]{5,4,3,2,1,0:T(8,128)(2,1)} %get-tuple-element.49), channel_id=1, source_target_pairs={{0,1},{1,0},{2,3},{3,2},{4,5},{5,4},{6,7},{7,6},{8,9},{9,8},{10,11... | collective-permute-start | bytes 2359304 | tf_op jit(solution)/shard_map/ppermute | solution.py:479
  91.8 19.9 %copy-start.20 = (bf16[2,2,2,192,128]{4,3,2,1,0:T(8,128)(2,1)S(1)}, bf16[2,2,2,192,128]{4,3,2,1,0:T(8,128)(2,1)}, u32[]{:S(2)}) copy-start(bf16[2,2,2,192,128]{4,3,2,1,0:T(8,128)(2,1)} %get-tuple-element.50) | copy-start | bytes 1179652
  91.8 12.9 %collective-permute-start.33 = (bf16[1,64,1792]{2,1,0:T(8,128)(2,1)S(1)}, bf16[1,64,1792]{2,1,0:T(8,128)(2,1)S(1)}, u32[]{:S(2)}, u32[]{:S(2)}) collective-permute-start(bf16[1,64,1792]{2,1,0:T(8,128)(2,1)S(1)} %bitcast_add_fusion.4), channel_id=1, source_target_pairs={{0,8},{2,10},{4,12},{6,14},{8,16},{10,18},{12,20},{14,22},{16,24},... | collective-permute-start | bytes 688136 | tf_op jit(solution)/shard_map/ppermute | solution.py:488
  104.6 9.6 %copy-start.6 = (bf16[192,1792]{1,0:T(8,128)(2,1)S(1)}, bf16[192,1792]{1,0:T(8,128)(2,1)}, u32[]{:S(2)}) copy-start(bf16[192,1792]{1,0:T(8,128)(2,1)} %copy-done.5) | copy-start | bytes 2064388
  104.6 9.6 %collective-permute-start.24 = (bf16[192,1792]{1,0:T(8,128)(2,1)}, bf16[192,1792]{1,0:T(8,128)(2,1)S(1)}, u32[]{:S(2)}, u32[]{:S(2)}) collective-permute-start(bf16[192,1792]{1,0:T(8,128)(2,1)} %collective-permute-done.1.other_ref.refs_4_), channel_id=1, source_target_pairs={{0,2},{2,0},{4,6},{6,4},{8,10},{10,8},{12,14},{14,12},{16,18},{18,... | collective-permute-start | bytes 2064392 | tf_op jit(solution)/shard_map/ppermute | solution.py:485
  104.7 10.5 %collective-permute-start.25 = (bf16[192,1792]{1,0:T(8,128)(2,1)}, bf16[192,1792]{1,0:T(8,128)(2,1)S(1)}, u32[]{:S(2)}, u32[]{:S(2)}) collective-permute-start(bf16[192,1792]{1,0:T(8,128)(2,1)} %collective-permute-done.23.refs_5_), channel_id=1, source_target_pairs={{0,2},{2,0},{4,6},{6,4},{8,10},{10,8},{12,14},{14,12},{16,18},{18,... | collective-permute-start | bytes 2064392 | tf_op jit(solution)/shard_map/ppermute | solution.py:485
  113.0 6.8 %copy-start.4 = (bf16[2,2,2,192,128]{4,3,2,1,0:T(8,128)(2,1)}, bf16[2,2,2,192,128]{4,3,2,1,0:T(8,128)(2,1)S(1)}, u32[]{:S(2)}) copy-start(bf16[2,2,2,192,128]{4,3,2,1,0:T(8,128)(2,1)S(1)} %get-tuple-element.71.refs_0_) | copy-start | bytes 1179652
  113.0 12.1 %collective-permute-start.5 = (bf16[2,2,2,192,128]{4,3,2,1,0:T(8,128)(2,1)S(1)}, bf16[2,2,2,192,128]{4,3,2,1,0:T(8,128)(2,1)S(1)}, u32[]{:S(2)}, u32[]{:S(2)}) collective-permute-start(bf16[2,2,2,192,128]{4,3,2,1,0:T(8,128)(2,1)S(1)} %get-tuple-element.70), channel_id=1, source_target_pairs={{0,4},{2,6},{4,0},{6,2},{8,12},{10,14},{12,8},{14,10},{16,20},{18,... | collective-permute-start | bytes 1179656 | tf_op jit(solution)/shard_map/ppermute | solution.py:482
  114.2 1.1 copy-start.16
  114.2 24.2 %collective-permute-start.9 = (bf16[192,1792]{1,0:T(8,128)(2,1)S(1)}, bf16[192,1792]{1,0:T(8,128)(2,1)}, u32[]{:S(2)}, u32[]{:S(2)}) collective-permute-start(bf16[192,1792]{1,0:T(8,128)(2,1)S(1)} %copy-done.6), channel_id=1, source_target_pairs={{0,4},{2,6},{4,0},{6,2},{8,12},{10,14},{12,8},{14,10},{16,20},{18,... | collective-permute-start | bytes 2064392 | tf_op jit(solution)/shard_map/ppermute | solution.py:482
  115.2 0.9 copy-start.17
  116.1 23.5 %collective-permute-start.6 = (bf16[2,2,192,128]{3,2,1,0:T(8,128)(2,1)S(1)}, bf16[2,2,192,128]{3,2,1,0:T(8,128)(2,1)S(1)}, u32[]{:S(2)}, u32[]{:S(2)}) collective-permute-start(bf16[2,2,192,128]{3,2,1,0:T(8,128)(2,1)S(1)} %slice_bitcast_fusion.3), channel_id=1, source_target_pairs={{0,2},{2,0},{4,6},{6,4},{8,10},{10,8},{12,14},{14,12},{16,18},{18,... | collective-permute-start | bytes 589832 | tf_op jit(solution)/shard_map/ppermute | solution.py:485
  125.1 17.3 %copy-start.9 = (bf16[2,2,2,192,128]{4,3,2,1,0:T(8,128)(2,1)}, bf16[2,2,2,192,128]{4,3,2,1,0:T(8,128)(2,1)S(1)}, u32[]{:S(2)}) copy-start(bf16[2,2,2,192,128]{4,3,2,1,0:T(8,128)(2,1)S(1)} %collective-permute-done.5.refs_1_) | copy-start | bytes 1179652
  125.1 6.6 %collective-permute-start.26 = (bf16[1,64,1792]{2,1,0:T(8,128)(2,1)S(1)}, bf16[1,64,1792]{2,1,0:T(8,128)(2,1)S(1)}, u32[]{:S(2)}, u32[]{:S(2)}) collective-permute-start(bf16[1,64,1792]{2,1,0:T(8,128)(2,1)S(1)} %dynamic-slice_bitcast_fusion.3), channel_id=1, source_target_pairs={{0,24},{2,26},{4,28},{6,30},{8,0},{10,2},{12,4},{14,6},{16,8},{18,... | collective-permute-start | bytes 688136 | tf_op jit(solution)/shard_map/ppermute | solution.py:488
  131.7 7.9 %collective-permute-start.7 = (bf16[2,2,192,128]{3,2,1,0:T(8,128)(2,1)S(1)}, bf16[2,2,192,128]{3,2,1,0:T(8,128)(2,1)S(1)}, u32[]{:S(2)}, u32[]{:S(2)}) collective-permute-start(bf16[2,2,192,128]{3,2,1,0:T(8,128)(2,1)S(1)} %slice_bitcast_fusion.2), channel_id=1, source_target_pairs={{0,2},{2,0},{4,6},{6,4},{8,10},{10,8},{12,14},{14,12},{16,18},{18,... | collective-permute-start | bytes 589832 | tf_op jit(solution)/shard_map/ppermute | solution.py:485
  132.7 21.0 %collective-permute-start.10 = (bf16[192,1792]{1,0:T(8,128)(2,1)S(1)}, bf16[192,1792]{1,0:T(8,128)(2,1)}, u32[]{:S(2)}, u32[]{:S(2)}) collective-permute-start(bf16[192,1792]{1,0:T(8,128)(2,1)S(1)} %copy-done.6), channel_id=1, source_target_pairs={{0,2},{2,0},{4,6},{6,4},{8,10},{10,8},{12,14},{14,12},{16,18},{18,... | collective-permute-start | bytes 2064392 | tf_op jit(solution)/shard_map/ppermute | solution.py:485
  133.3 68.8 %collective-permute-start.2 = (bf16[192,1792]{1,0:T(8,128)(2,1)}, bf16[192,1792]{1,0:T(8,128)(2,1)}, u32[]{:S(2)}, u32[]{:S(2)}) collective-permute-start(bf16[192,1792]{1,0:T(8,128)(2,1)} %input_other.1), channel_id=1, source_target_pairs={{0,1},{1,0},{2,3},{3,2},{4,5},{5,4},{6,7},{7,6},{8,9},{9,8},{10,11... | collective-permute-start | bytes 2064392 | tf_op jit(solution)/shard_map/ppermute | solution.py:479
  138.4 65.7 %collective-permute-start.34 = (bf16[1,64,1792]{2,1,0:T(8,128)(2,1)}, bf16[1,64,1792]{2,1,0:T(8,128)(2,1)}, u32[]{:S(2)}, u32[]{:S(2)}) collective-permute-start(bf16[1,64,1792]{2,1,0:T(8,128)(2,1)} %bitcast_add_fusion.5), channel_id=1, source_target_pairs={{0,8},{2,10},{4,12},{6,14},{8,16},{10,18},{12,20},{14,22},{16,24},... | collective-permute-start | bytes 688136 | tf_op jit(solution)/shard_map/ppermute | solution.py:488
  139.6 2.8 %copy-start.12 = (bf16[2,2,192,128]{3,2,1,0:T(8,128)(2,1)}, bf16[2,2,192,128]{3,2,1,0:T(8,128)(2,1)S(1)}, u32[]{:S(2)}) copy-start(bf16[2,2,192,128]{3,2,1,0:T(8,128)(2,1)S(1)} %collective-permute-done.6.refs_2_) | copy-start | bytes 589828
  139.6 17.4 %collective-permute-start.11 = (bf16[192,1792]{1,0:T(8,128)(2,1)}, bf16[192,1792]{1,0:T(8,128)(2,1)}, u32[]{:S(2)}, u32[]{:S(2)}) collective-permute-start(bf16[192,1792]{1,0:T(8,128)(2,1)} %collective-permute-done.9.refs_5_), channel_id=1, source_target_pairs={{0,2},{2,0},{4,6},{6,4},{8,10},{10,8},{12,14},{14,12},{16,18},{18,... | collective-permute-start | bytes 2064392 | tf_op jit(solution)/shard_map/ppermute | solution.py:485
  139.6 2.8 %copy-start.13 = (bf16[2,2,192,128]{3,2,1,0:T(8,128)(2,1)}, bf16[2,2,192,128]{3,2,1,0:T(8,128)(2,1)S(1)}, u32[]{:S(2)}) copy-start(bf16[2,2,192,128]{3,2,1,0:T(8,128)(2,1)S(1)} %collective-permute-done.7.refs_3_) | copy-start | bytes 589828
  139.6 11.9 %collective-permute-start.27 = (bf16[1,64,1792]{2,1,0:T(8,128)(2,1)S(1)}, bf16[1,64,1792]{2,1,0:T(8,128)(2,1)S(1)}, u32[]{:S(2)}, u32[]{:S(2)}) collective-permute-start(bf16[1,64,1792]{2,1,0:T(8,128)(2,1)S(1)} %bitcast_add_fusion.6), channel_id=1, source_target_pairs={{0,24},{2,26},{4,28},{6,30},{8,0},{10,2},{12,4},{14,6},{16,8},{18,... | collective-permute-start | bytes 688136 | tf_op jit(solution)/shard_map/ppermute | solution.py:488
  151.5 15.4 %collective-permute-start.18 = (bf16[2,64,1792]{2,1,0:T(8,128)(2,1)S(1)}, bf16[2,64,1792]{2,1,0:T(8,128)(2,1)}, u32[]{:S(2)}, u32[]{:S(2)}) collective-permute-start(bf16[2,64,1792]{2,1,0:T(8,128)(2,1)S(1)} %dynamic-slice_bitcast_fusion), channel_id=1, source_target_pairs={{0,8},{2,10},{4,12},{6,14},{8,16},{10,18},{12,20},{14,22},{16,24},... | collective-permute-start | bytes 1376264 | tf_op jit(solution)/shard_map/ppermute | solution.py:488
  153.7 13.2 %copy-start = (bf16[4,2,64,1792]{3,2,1,0:T(8,128)(2,1)S(1)}, bf16[4,2,64,1792]{3,2,1,0:T(8,128)(2,1)}, u32[]{:S(2)}) copy-start(bf16[4,2,64,1792]{3,2,1,0:T(8,128)(2,1)} %shard_map.112.partial_ref) | copy-start | bytes 5505028
  153.7 54.0 %collective-permute-start.28 = (bf16[1,64,1792]{2,1,0:T(8,128)(2,1)}, bf16[1,64,1792]{2,1,0:T(8,128)(2,1)}, u32[]{:S(2)}, u32[]{:S(2)}) collective-permute-start(bf16[1,64,1792]{2,1,0:T(8,128)(2,1)} %bitcast_add_fusion.7), channel_id=1, source_target_pairs={{0,24},{2,26},{4,28},{6,30},{8,0},{10,2},{12,4},{14,6},{16,8},{18,... | collective-permute-start | bytes 688136 | tf_op jit(solution)/shard_map/ppermute | solution.py:488
  161.9 19.7 %copy-start.1 = (bf16[4,2,64,1792]{3,2,1,0:T(8,128)(2,1)S(1)}, bf16[4,2,64,1792]{3,2,1,0:T(8,128)(2,1)}, u32[]{:S(2)}) copy-start(bf16[4,2,64,1792]{3,2,1,0:T(8,128)(2,1)} %shard_map.111.partial_ref) | copy-start | bytes 5505028
  163.1 18.5 %collective-permute-start.12 = (bf16[2,64,1792]{2,1,0:T(8,128)(2,1)S(1)}, bf16[2,64,1792]{2,1,0:T(8,128)(2,1)S(1)}, u32[]{:S(2)}, u32[]{:S(2)}) collective-permute-start(bf16[2,64,1792]{2,1,0:T(8,128)(2,1)S(1)} %dynamic-slice_bitcast_fusion.1), channel_id=1, source_target_pairs={{0,24},{2,26},{4,28},{6,30},{8,0},{10,2},{12,4},{14,6},{16,8},{18,... | collective-permute-start | bytes 1376264 | tf_op jit(solution)/shard_map/ppermute | solution.py:488
  168.0 34.1 %copy-start.3 = (f32[192,1792]{1,0:T(8,128)S(1)}, f32[192,1792]{1,0:T(8,128)}, u32[]{:S(2)}) copy-start(f32[192,1792]{1,0:T(8,128)} %input_own.1) | copy-start | bytes 4128772
  168.0 23.4 %collective-permute-start.19 = (bf16[2,64,1792]{2,1,0:T(8,128)(2,1)S(1)}, bf16[2,64,1792]{2,1,0:T(8,128)(2,1)S(1)}, u32[]{:S(2)}, u32[]{:S(2)}) collective-permute-start(bf16[2,64,1792]{2,1,0:T(8,128)(2,1)S(1)} %bitcast_add_fusion), channel_id=1, source_target_pairs={{0,8},{2,10},{4,12},{6,14},{8,16},{10,18},{12,20},{14,22},{16,24},... | collective-permute-start | bytes 1376264 | tf_op jit(solution)/shard_map/ppermute | solution.py:488
  181.6 19.6 %collective-permute-start.13 = (bf16[2,64,1792]{2,1,0:T(8,128)(2,1)S(1)}, bf16[2,64,1792]{2,1,0:T(8,128)(2,1)S(1)}, u32[]{:S(2)}, u32[]{:S(2)}) collective-permute-start(bf16[2,64,1792]{2,1,0:T(8,128)(2,1)S(1)} %bitcast_add_fusion.2), channel_id=1, source_target_pairs={{0,24},{2,26},{4,28},{6,30},{8,0},{10,2},{12,4},{14,6},{16,8},{18,... | collective-permute-start | bytes 1376264 | tf_op jit(solution)/shard_map/ppermute | solution.py:488
  191.4 20.0 %collective-permute-start.20 = (bf16[2,64,1792]{2,1,0:T(8,128)(2,1)S(1)}, bf16[2,64,1792]{2,1,0:T(8,128)(2,1)S(1)}, u32[]{:S(2)}, u32[]{:S(2)}) collective-permute-start(bf16[2,64,1792]{2,1,0:T(8,128)(2,1)S(1)} %bitcast_add_fusion.1), channel_id=1, source_target_pairs={{0,8},{2,10},{4,12},{6,14},{8,16},{10,18},{12,20},{14,22},{16,24},... | collective-permute-start | bytes 1376264 | tf_op jit(solution)/shard_map/ppermute | solution.py:488
  201.3 18.8 %collective-permute-start.14 = (bf16[2,64,1792]{2,1,0:T(8,128)(2,1)S(1)}, bf16[2,64,1792]{2,1,0:T(8,128)(2,1)S(1)}, u32[]{:S(2)}, u32[]{:S(2)}) collective-permute-start(bf16[2,64,1792]{2,1,0:T(8,128)(2,1)S(1)} %bitcast_add_fusion.3), channel_id=1, source_target_pairs={{0,24},{2,26},{4,28},{6,30},{8,0},{10,2},{12,4},{14,6},{16,8},{18,... | collective-permute-start | bytes 1376264 | tf_op jit(solution)/shard_map/ppermute | solution.py:488
  211.4 0.8 copy-start.19
  220.0 0.8 copy-start.18
where the time goes:
time: 227 us; the launch traced here: 225 us
  Pallas kernels  85.3 us (38%)
  waiting for transfers between devices  80.2 us (35%)
  starting transfers between devices  37.6 us (17%)
  other arithmetic  12.9 us (6%)
  local copies, waits for them, and re-layouts  7.38 us (3%)
    ppermute x12, waiting for transfers between devices, ring(): lax.ppermute(v, 'dp', [(i, (i + step * inner) % replicas) for i in range(...  46.4 us
    ppermute x12, starting transfers between devices, ring(): lax.ppermute(v, 'dp', [(i, (i + step * inner) % replicas) for i in range(...  19.3 us
    pallas_call x2, Pallas kernels, input_part(): pl.pallas_call(body, out_shape=jax.ShapeDtypeStruct((rows, half), jnp.bfl...  18.5 us
    ppermute x5, waiting for transfers between devices, over_y(): return lax.ppermute(v, 'tp', tp_swap)  18.2 us
    pallas_call x4, Pallas kernels, weight_grad(): pl.pallas_call(body, out_shape=jax.ShapeDtypeStruct((2 * quarter, kinds,...  17.2 us
    pallas_call x4, Pallas kernels, adam(): pl.pallas_call(body, out_shape=(jax.ShapeDtypeStruct(master.shape, jnp.fl...  15.7 us
    ppermute x6, waiting for transfers between devices, over_x(): return lax.ppermute(v, 'dp', x_swap)  15.7 us
    pallas_call x1, Pallas kernels, own_part(): pl.pallas_call(body, out_shape=(out,) * 3, grid_spec=pltpu.PrefetchScalar...  12.2 us
  transfers between devices with their start and end apart: 35, of which 12 were waited for; matrix products, arithmetic and copies ran while one was open for 8% of the time, Pallas kernels for 36%

commit v1 on v0

--- a/solution.py
+++ b/solution.py
@@ -364,94 +364,110 @@
     )(scalars, grads, *[working] * 4)
 
 
-def weight_grad(acts, inputs):
+def weight_grad(acts, inputs, kind, own):
     group = len(acts)
-    quarter, kinds, rows, _ = acts[0].shape[-4:]
+    quarter, _, rows, _ = acts[0].shape[-4:]
     half = inputs[0].shape[1]
     narrow = BLOCK // CORES
     wide = quarter * BLOCK
+    owners = PAIR * quarter
     tile = half // 2 if half % (2 * BLOCK) == 0 else half
 
-    def body(*refs):
-        a_refs, x_refs = refs[:group], refs[group : 2 * group]
-        out_ref, left = refs[2 * group :]
+    def body(s, *refs):
+        a_refs, x_refs, outs = refs[:group], refs[group : 2 * group], refs[2 * group : 2 * group + owners]
+        left, value = refs[2 * group + owners :]
 
         @pl.when(pl.program_id(0) == 0)
         def _():
-            for kind in range(kinds):
-                for p in range(quarter):
-                    column = jnp.concatenate(
-                        [ref[0, p, kind] if len(ref.shape) == 5 else ref[p, kind] for ref in a_refs], axis=0
-                    )
-                    left[kind, p * BLOCK : (p + 1) * BLOCK, :] = column.T
+            for p in range(quarter):
+                column = jnp.concatenate(
+                    [ref[0, p, 0] if len(ref.shape) == 5 else ref[p, 0] for ref in a_refs], axis=0
+                )
+                left[p * BLOCK : (p + 1) * BLOCK, :] = column.T
 
         right = jnp.concatenate([ref[...] for ref in x_refs], axis=0)
-        for kind in range(kinds):
-            value = dot32(left[kind], right, contract_mid).astype(jnp.bfloat16)
-            for z in range(2 * quarter):
-                out_ref[z, kind] = value[z * narrow : (z + 1) * narrow]
+        value[...] = dot32(left[...], right, contract_mid).astype(jnp.bfloat16)
+        for relation, out_ref in enumerate(outs):
+            start = pl.multiple_of(jnp.bitwise_xor(s[0], relation) * narrow, narrow)
+            out_ref[...] = value[pl.ds(start, narrow), :]
 
     def act_spec(a):
         if a.ndim == 5:
-            return pl.BlockSpec((1, *a.shape[1:]), lambda i: (0,) * 5)
-        return pl.BlockSpec(a.shape, lambda i: (0,) * 4)
-
+            return pl.BlockSpec((1, quarter, 1, rows, BLOCK), lambda i, s: (0, 0, kind, 0, 0))
+        return pl.BlockSpec((quarter, 1, rows, BLOCK), lambda i, s: (0, kind, 0, 0))
+
+    out = jax.ShapeDtypeStruct((narrow, half), jnp.bfloat16)
     return pl.pallas_call(
         body,
-        out_shape=jax.ShapeDtypeStruct((2 * quarter, kinds, narrow, half), jnp.bfloat16),
-        grid=(half // tile,),
-        in_specs=[act_spec(a) for a in acts] + [pl.BlockSpec((rows, tile), lambda i: (0, i))] * group,
-        out_specs=pl.BlockSpec((2 * quarter, kinds, narrow, tile), lambda i: (0, 0, 0, i)),
-        scratch_shapes=[pltpu.VMEM((kinds, wide, group * rows), jnp.bfloat16)],
+        out_shape=(out,) * owners,
+        grid_spec=pltpu.PrefetchScalarGridSpec(
+            num_scalar_prefetch=1,
+            grid=(half // tile,),
+            in_specs=[act_spec(a) for a in acts] + [pl.BlockSpec((rows, tile), lambda i, s: (0, i))] * group,
+            out_specs=(pl.BlockSpec((narrow, tile), lambda i, s: (0, i)),) * owners,
+            scratch_shapes=[
+                pltpu.VMEM((wide, group * rows), jnp.bfloat16),
+                pltpu.VMEM((wide, tile), jnp.bfloat16),
+            ],
+        ),
         cost_estimate=pl.CostEstimate(
-            flops=2 * kinds * group * rows * wide * half,
-            bytes_accessed=2 * group * rows * half + 2 * kinds * wide * half,
+            flops=2 * group * rows * wide * half,
+            bytes_accessed=2 * group * rows * half + 2 * wide * half,
             transcendentals=0,
         ),
-    )(*acts, *inputs)
-
-
-def adam(place, arrived, partial, first, master, moment_one, moment_two, before, replicas):
-    _, kinds, rows, half = partial.shape
-    step = rows
-    state = pl.BlockSpec((1, step, half), lambda k, i, s: (k + first, i, s[1]))
-
-    def body(s, arrived_ref, partial_ref, master_ref, one_ref, two_ref, *refs):
+    )(own, *acts, *inputs)
+
+
+def adam(me, sums, kinds, halves, master, moment_one, moment_two, before, replicas):
+    rows, half = sums[0][0].shape
+    count = len(sums[0])
+    steps = len(sums)
+    columns = master.shape[2] // half
+
+    def at(i, s):
+        kind = kinds[0] + i * (kinds[1] - kinds[0])
+        return (kind, 0, (s[0] + halves[0] + i * (halves[1] - halves[0])) % columns)
+
+    state = pl.BlockSpec((1, rows, half), at)
+
+    def body(s, *refs):
+        parts, (master_ref, one_ref, two_ref) = refs[: steps * count], refs[steps * count : steps * count + 3]
         master_out, one_out, two_out = refs[-3:]
-        summed = arrived_ref[0].astype(jnp.float32) + partial_ref[0, 0].astype(jnp.float32)
-        grad_mean = summed * (1.0 / replicas)
-        one = beta_one * one_ref[0] + (1.0 - beta_one) * grad_mean
-        two = beta_two * two_ref[0] + (1.0 - beta_two) * grad_mean * grad_mean
-        old = master_ref[0]
-        update = one * (1.0 / bias_one) / (jnp.sqrt(two * (1.0 / bias_two)) + adam_eps) + decay_rate * old
-        master_out[0] = old - learn_rate * update
-        one_out[0] = one
-        two_out[0] = two
-
-    aliases = {} if before is None else {6: 0, 7: 1, 8: 2}
+        for i in range(steps):
+
+            @pl.when(pl.program_id(0) == i)
+            def _(i=i):
+                summed = parts[i * count][...].astype(jnp.float32)
+                for part in parts[i * count + 1 : (i + 1) * count]:
+                    summed = summed + part[...].astype(jnp.float32)
+                grad_mean = summed * (1.0 / replicas)
+                one = beta_one * one_ref[0] + (1.0 - beta_one) * grad_mean
+                two = beta_two * two_ref[0] + (1.0 - beta_two) * grad_mean * grad_mean
+                old = master_ref[0]
+                update = one * (1.0 / bias_one) / (jnp.sqrt(two * (1.0 / bias_two)) + adam_eps) + decay_rate * old
+                master_out[0] = old - learn_rate * update
+                one_out[0] = one
+                two_out[0] = two
+
     extra = () if before is None else before
+    flat = [part for group in sums for part in group]
     return pl.pallas_call(
         body,
         out_shape=(jax.ShapeDtypeStruct(master.shape, jnp.float32),) * 3,
         grid_spec=pltpu.PrefetchScalarGridSpec(
             num_scalar_prefetch=1,
-            grid=(kinds, rows // step),
-            in_specs=[
-                pl.BlockSpec((1, step, half), lambda k, i, s: (k, i, 0)),
-                pl.BlockSpec((1, 1, step, half), lambda k, i, s: (s[0], k, i, 0)),
-                state,
-                state,
-                state,
-            ]
+            grid=(steps,),
+            in_specs=[pl.BlockSpec((rows, half), lambda i, s: (0, 0))] * len(flat)
+            + [state] * 3
             + [pl.BlockSpec(memory_space=pl.ANY)] * len(extra),
-            out_specs=(state, state, state),
-        ),
-        input_output_aliases=aliases,
+            out_specs=(state,) * 3,
+        ),
+        input_output_aliases={len(flat) + 4 + i: i for i in range(len(extra))},
         cost_estimate=pl.CostEstimate(
-            flops=20 * kinds * rows * half, bytes_accessed=28 * kinds * rows * half, transcendentals=0
+            flops=20 * steps * rows * half, bytes_accessed=28 * steps * rows * half, transcendentals=0
         ),
         name="adam",
-    )(place, arrived, partial, master, moment_one, moment_two, *extra)
+    )(me, *flat, master, moment_one, moment_two, *extra)
 
 
 def grouped(*args):
@@ -461,37 +477,37 @@
 def grouped_step(tokens, cotangent, working, degraded, block_map, master, moment_one, moment_two):
     replicas = lax.axis_size("dp")
     tp_size = lax.axis_size("tp")
-    inner = 2 * CORES
-    depth = replicas // inner
     me = lax.axis_index("tp")
     mine = lax.axis_index("dp")
-    z, x, core = mine // inner, (mine // CORES) % 2, mine % CORES
+    core, x = mine % CORES, (mine // CORES) % 2
+    zs, zp = (mine // (2 * CORES)) % 2, mine // (4 * CORES)
     slot_count = working.shape[3] // BLOCK
     per_dev = BLOCKS // tp_size
     half = tokens.shape[1]
-
-    tp_swap = [(i, (i + 1) % tp_size) for i in range(tp_size)]
-    x_swap = [(i, i ^ CORES) for i in range(replicas)]
-    core_swap = [(i, i ^ 1) for i in range(replicas)]
     after = lax.optimization_barrier
 
     def over_y(v):
-        return lax.ppermute(v, "tp", tp_swap)
+        return lax.ppermute(v, "tp", [(i, (i + 1) % tp_size) for i in range(tp_size)])
+
+    def over(bit, v):
+        pairs = [(i, i ^ bit) for i in range(replicas)]
+        return lax.ppermute(v, "dp", pairs)
+
+    def over_core(v):
+        return over(1, v)
 
     def over_x(v):
-        return lax.ppermute(v, "dp", x_swap)
-
-    def over_core(v):
-        return lax.ppermute(v, "dp", core_swap)
-
-    def ring(v, step):
-        return lax.ppermute(v, "dp", [(i, (i + step * inner) % replicas) for i in range(replicas)])
+        return over(CORES, v)
+
+    def over_s(v):
+        return over(2 * CORES, v)
+
+    def over_m(v):
+        return over(4 * CORES, v)
 
     order = jnp.arange(BLOCKS, dtype=jnp.int32)
-    along = order % depth
-    far_x = 1 - (order // depth) % 2
-    far_y = 1 - order // per_dev
-    block = ((me + far_y) % tp_size) * per_dev + along * 2 + (x ^ far_x)
+    far_y, far_s = 1 - order // per_dev, 1 - (order // 4) % 2
+    block = ((me + far_y) % tp_size) * per_dev + ((order // 2) % 2) * 4 + (zs ^ far_s) * 2 + order % 2
     places = layout_places(degraded[0], block_map[0], tp_size, slot_count)
     blocks = jnp.arange(BLOCKS, dtype=jnp.int32)
     place = jnp.sum(jnp.where(block[:, None] == blocks[None, :], places[None, :], 0), axis=1)
@@ -499,11 +515,12 @@
     slots = jnp.where(held, place % slot_count, 0)
     extra = jnp.where(blocks == 0, me, jnp.where(blocks == 1, core, 0))
     scalars = jnp.concatenate([slots, held.astype(jnp.int32), extra.astype(jnp.int32)])
+    own = (zp * 2 + x).astype(jnp.int32).reshape(1)
 
     t_own, c_own = tokens, cotangent
     t_other = over_y(t_own)
-    c_own_x = over_x(c_own)
-    t_own_x = over_x(t_own)
+    c_own_s = over_s(c_own)
+    t_own_s = over_s(t_own)
     gate, up, down = own_part(scalars, t_own, c_own, working)
     t_other, c_first = after((t_other, c_own))
     c_other = over_y(c_first)
@@ -511,60 +528,67 @@
     act, slope, h_theirs, h_far, h_near = gate_up(scalars, t_other, working, gate, up)
     c_other, h_theirs = after((c_other, h_theirs))
     h_from = over_y(h_theirs)
-    c_other_x = over_x(c_other)
+    c_other_s = over_s(c_other)
     grads, d_theirs, d_far, d_near = down_acts(scalars, c_other, working, down, act, slope)
     h_from, d_theirs = after((h_from, d_theirs))
     d_from = over_y(d_theirs)
 
     def spread(far, near, came):
         far = far + came[0]
-        near_x = over_x(far)
+        near_s = over_s(far)
         near = near + came[1]
-        return [near, near_x, over_core(near[1]), over_core(near_x[1])]
+        return [near, near_s, over_core(near[1]), over_core(near_s[1])]
 
     hidden_acts = spread(h_far, h_near, h_from)
     c_acts = [
-        [c_own, c_own_x, c_own_c, over_core(c_own_x)], [c_other, c_other_x, over_core(c_other), over_core(c_other_x)]
+        [c_own, c_own_s, c_own_c, over_core(c_own_s)], [c_other, c_other_s, over_core(c_other), over_core(c_other_s)]
     ]
     hidden_acts[1], t_late = after((hidden_acts[1], t_other))
-    t_other_x = over_x(t_late)
+    t_other_s = over_s(t_late)
     t_acts = [
-        [t_own, t_own_x, t_own_c, over_core(t_own_x)], [t_other, t_other_x, over_core(t_other), over_core(t_other_x)]
+        [t_own, t_own_s, t_own_c, over_core(t_own_s)], [t_other, t_other_s, over_core(t_other), over_core(t_other_s)]
     ]
-
-    parts = [(2, h, weight_grad(hidden_acts, c_acts[h])) for h in range(2)]
     grad_acts = spread(d_far, d_near, d_from)
-    parts += [(0, h, weight_grad(grad_acts, t_acts[h])) for h in range(2)]
-    steps = (1, -1)
-    moving = [None] * len(parts)
-    for low in (0, 2):
-        for s in range(1, depth):
-            for at in (low, low + 1):
-                _, h, partial = parts[at]
-                chunk = lax.dynamic_index_in_dim(partial, (z - steps[h] * s) % depth, 0, keepdims=False)
-                chunk = chunk if moving[at] is None else chunk + moving[at]
-                moving[at] = ring(chunk, steps[h])
+
+    sums = []
+    for kind, h in PIECES:
+        acts, inputs = (hidden_acts, c_acts[h]) if kind == 2 else (grad_acts, t_acts[h])
+        keep, far_x, far_z, far_both = weight_grad(acts, inputs, kind % 2, own)
+        came = over_x(far_both)
+        far_z = far_z + came
+        sums.append((keep, over_x(far_x), over_m(far_z)))
+    state = None
+    for at in range(0, len(PIECES), 2):
+        kinds, halves = zip(*PIECES[at : at + 2])
+        state = adam(
+            me.astype(jnp.int32).reshape(1),
+            sums[at : at + 2],
+            kinds,
+            halves,
+            master,
+            moment_one,
+            moment_two,
+            state,
+            replicas,
+        )
 
     sent = over_y(input_part(scalars, grads, working, half, 1))
     kept = input_part(scalars, grads, working, half, 0)
     input_grad = (kept + sent.astype(jnp.float32)).astype(jnp.bfloat16)
-
-    state = None
-    for (first, h, partial), arrived in zip(parts, moving):
-        where = jnp.stack([z, (me + h) % tp_size]).astype(jnp.int32)
-        state = adam(where, arrived, partial, first, master, moment_one, moment_two, state, replicas)
     return (input_grad, *state)
+
+
+PIECES = ((2, 0), (2, 1), (0, 0), (1, 0), (0, 1), (1, 1))
 
 
 def solution(mesh):
     replicas, tp_size = mesh.shape["dp"], mesh.shape["tp"]
-    inner = 2 * CORES
 
     def per_part(*args):
         half = args[0].shape[1]
         rows = args[5].shape[1]
         aligned = half % BLOCK == 0 and args[0].shape[0] % 16 == 0 and rows * CORES == BLOCK
-        split = replicas % (2 * inner) == 0 and tp_size == 2 and BLOCKS == tp_size * replicas // CORES
+        split = replicas == 8 * CORES and tp_size == 2 and BLOCKS == tp_size * replicas // CORES
         return (grouped if aligned and split else per_device)(*args)
 
     return jax.shard_map(

time: 227 us -> 212 us (0.934)
  waiting for transfers between devices: 80.2 us -> 68.4 us
  other arithmetic: 12.9 us -> 10.2 us
  local copies, waits for them, and re-layouts: 7.38 us -> 4.9 us
    ppermute x35 -> x41, waiting for transfers between devices: 80.2 us -> 68.4 us  [the longest x36 46.7 us: over(): return lax.ppermute(v, 'dp', pairs)]
    pallas_call x4 -> x6, Pallas kernels: 17.2 us -> 22.3 us  [weight_grad(): pl.pallas_call(body, out_shape=(out,) * owners, grid_spec=pltpu.PrefetchS...]
    pallas_call x4 -> x3, Pallas kernels: 15.7 us -> 12 us  [adam(): pl.pallas_call(body, out_shape=(jax.ShapeDtypeStruct(master.shape, jnp.fl...]
    add x8 -> x7, other arithmetic: 4.59 us -> 2.43 us  [the longest x6 2.41 us: grouped_step(): far_z = far_z + came]
    ppermute x35 -> x41, starting transfers between devices: 37.6 us -> 38.5 us  [the longest x36 34.6 us: over(): return lax.ppermute(v, 'dp', pairs)]
  transfers between devices with their start and end apart: 35 -> 41, of which waited for: 12 -> 13; matrix products, arithmetic and copies ran while one was open for 8% -> 6% of each run, Pallas kernels for 36% -> 39%
where the time goes in v1:
time: 212 us; the launch traced here: 210 us
  Pallas kernels  86.6 us (41%)
  waiting for transfers between devices  68.4 us (32%)
  starting transfers between devices  38.5 us (18%)
  other arithmetic  10.2 us (5%)
  local copies, waits for them, and re-layouts  4.9 us (2%)
    ppermute x36, waiting for transfers between devices, over(): return lax.ppermute(v, 'dp', pairs)  46.7 us
    ppermute x36, starting transfers between devices, over(): return lax.ppermute(v, 'dp', pairs)  34.6 us
    pallas_call x6, Pallas kernels, weight_grad(): pl.pallas_call(body, out_shape=(out,) * owners, grid_spec=pltpu.PrefetchS...  22.3 us
    ppermute x5, waiting for transfers between devices, over_y(): lax.ppermute(v, 'tp', [(i, (i + 1) % tp_size) for i in range(tp_size)])  21.7 us
    pallas_call x2, Pallas kernels, input_part(): pl.pallas_call(body, out_shape=jax.ShapeDtypeStruct((rows, half), jnp.bfl...  18.4 us
    pallas_call x1, Pallas kernels, own_part(): pl.pallas_call(body, out_shape=(out,) * 3, grid_spec=pltpu.PrefetchScalar...  12.2 us
    pallas_call x3, Pallas kernels, adam(): pl.pallas_call(body, out_shape=(jax.ShapeDtypeStruct(master.shape, jnp.fl...  12 us
    pallas_call x1, Pallas kernels, gate_up(): pl.pallas_call(body, out_shape=(out, out, *shapes), grid_spec=pltpu.Prefe...  11.5 us
  transfers between devices with their start and end apart: 41, of which 13 were waited for; matrix products, arithmetic and copies ran while one was open for 6% of the time, Pallas kernels for 39%

profile of v1, /device:TPU:0, one launch (start us, length us, event | category | flops | bytes accessed | tf_op | source)
XLA Modules:
  0.0 210.4 jit_solution(13212756574088493545)
XLA Ops:
  0.6 3.1 %collective-permute-start.29 = (bf16[192,1792]{1,0:T(8,128)(2,1)}, bf16[192,1792]{1,0:T(8,128)(2,1)}, u32[]{:S(2)}, u32[]{:S(2)}) collective-permute-start(bf16[192,1792]{1,0:T(8,128)(2,1)} %refs_4_.7), channel_id=1, source_target_pairs={{0,8},{2,10},{4,12},{6,14},{8,0},{10,2},{12,4},{14,6},{16,24},{18,... | collective-permute-start | bytes 2064392 | tf_op jit(solution)/shard_map/ppermute | solution.py:494
  3.8 1.5 collective-permute-start
  5.9 0.7 broadcast_select_fusion
  7.1 14.7 %collective-permute-done.other_ref.refs_4_ = bf16[192,1792]{1,0:T(8,128)(2,1)S(1)} collective-permute-done((bf16[192,1792]{1,0:T(8,128)(2,1)}, bf16[192,1792]{1,0:T(8,128)(2,1)S(1)}, u32[]{:S(2)}, u32[]{:S(2)}) %collective-permute-start) | collective-permute-done | bytes 688160 | tf_op jit(solution)/shard_map/ppermute | solution.py:490
  21.8 1.5 collective-permute-start.1
  23.3 0.6 pad_add_fusion.s
  23.9 12.2 %own_part.1 = (f32[8,192,256]{2,1,0:T(8,128)}, f32[8,192,256]{2,1,0:T(8,128)}, f32[8,192,256]{2,1,0:T(8,128)}) custom-call(s32[48]{0:T(128)} %pad_add_fusion.s, bf16[192,1792]{1,0:T(8,128)(2,1)} %refs_4_.6, bf16[192,1792]{1,0:T(8,128)(2,1)} %refs_4_.7, bf16[1,1,3,2048,3584]{4,3,2,1,0:T(8,128)(2,1)} %w3.5, bf16[1,1,3,2048,3584]{4,3,2,1,0:T(8,128)(2,1)} %w3.5, ...), custom_call_target="tpu_custom_call" | custom-call | flops 4227858432 | bytes 22020096 | tf_op jit(solution)/shard_map/own_part/pallas_call | solution.py:160
  36.1 11.5 %gate_up.1 = (f32[8,192,256]{2,1,0:T(8,128)}, f32[8,192,256]{2,1,0:T(8,128)}, bf16[2,2,2,1,192,128]{5,4,3,2,1,0:T(8,128)(2,1)}, bf16[2,2,1,192,128]{4,3,2,1,0:T(8,128)(2,1)}, bf16[2,2,1,192,128]{4,3,2,1,0:T(8,128)(2,1)}) custom-call(s32[48]{0:T(128)} %pad_add_fusion.s, bf16[192,1792]{1,0:T(8,128)(2,1)} %copy-done.2, bf16[1,1,3,2048,3584]{4,3,2,1,0:T(8,128)(2,1)} %w3.5, ...), custom_call_target="tpu_custom_call" | custom-call | flops 2818572288 | bytes 20971520 | tf_op jit(solution)/shard_map/gate_up/pallas_call | solution.py:263
  47.6 0.5 collective-permute-start.3
  48.1 6.1 %collective-permute-start.18 = (bf16[192,1792]{1,0:T(8,128)(2,1)S(1)}, bf16[192,1792]{1,0:T(8,128)(2,1)S(1)}, u32[]{:S(2)}, u32[]{:S(2)}) collective-permute-start(bf16[192,1792]{1,0:T(8,128)(2,1)S(1)} %copy-done.4), channel_id=1, source_target_pairs={{0,8},{2,10},{4,12},{6,14},{8,0},{10,2},{12,4},{14,6},{16,24},{18,... | collective-permute-start | bytes 2064392 | tf_op jit(solution)/shard_map/ppermute | solution.py:494
  54.2 0.5 collective-permute-start.31
  54.7 10.1 %down_acts.1 = (bf16[8,2,192,256]{3,2,1,0:T(8,128)(2,1)}, bf16[2,2,2,2,192,128]{5,4,3,2,1,0:T(8,128)(2,1)}, bf16[2,2,2,192,128]{4,3,2,1,0:T(8,128)(2,1)}, bf16[2,2,2,192,128]{4,3,2,1,0:T(8,128)(2,1)}) custom-call(s32[48]{0:T(128)} %pad_add_fusion.s, bf16[192,1792]{1,0:T(8,128)(2,1)} %copy-done.14, bf16[1,1,3,2048,3584]{4,3,2,1,0:T(8,128)(2,1)} %w3.5, ...), custom_call_target="tpu_custom_call" | custom-call | flops 1409286144 | bytes 15204352 | tf_op jit(solution)/shard_map/down_acts/pallas_call | solution.py:308
  65.0 1.0 bitcast_add_fusion.1
  66.1 1.9 collective-permute-start.8
  68.0 1.0 bitcast_add_fusion
  69.0 1.5 collective-permute-done.18.refs_5_
  70.5 4.1 %collective-permute-done.8 = bf16[2,2,1,192,128]{4,3,1,2,0:T(8,128)(2,1)S(1)} collective-permute-done((bf16[2,2,1,192,128]{4,3,1,2,0:T(8,128)(2,1)S(1)}, bf16[2,2,1,192,128]{4,3,1,2,0:T(8,128)(2,1)S(1)}, u32[]{:S(2)}, u32[]{:S(2)}) %collective-permute-start.8) | collective-permute-done | bytes 196640 | tf_op jit(solution)/shard_map/ppermute | solution.py:494
  75.0 1.8 collective-permute-start.9
  76.8 0.6 slice_bitcast_fusion.4
  77.4 7.0 %collective-permute-done.4 = bf16[2,2,2,2,192,128]{5,4,3,2,1,0:T(8,128)(2,1)S(1)} collective-permute-done((bf16[2,2,2,2,192,128]{5,4,3,2,1,0:T(8,128)(2,1)}, bf16[2,2,2,2,192,128]{5,4,3,2,1,0:T(8,128)(2,1)S(1)}, u32[]{:S(2)}, u32[]{:S(2)}) %collective-permute-start.4) | collective-permute-done | bytes 786464 | tf_op jit(solution)/shard_map/ppermute | solution.py:490
  84.4 1.9 fusion
  86.3 0.6 collective-permute-start.28
  86.9 6.4 %collective-permute-done.35.refs_5_ = bf16[192,1792]{1,0:T(8,128)(2,1)} collective-permute-done((bf16[192,1792]{1,0:T(8,128)(2,1)}, bf16[192,1792]{1,0:T(8,128)(2,1)}, u32[]{:S(2)}, u32[]{:S(2)}) %collective-permute-start.35) | collective-permute-done | bytes 688160 | tf_op jit(solution)/shard_map/ppermute | solution.py:494
  93.3 0.6 copy-done.17
  94.2 9.1 %input_other.1 = bf16[192,1792]{1,0:T(8,128)(2,1)} custom-call(s32[48]{0:T(128)} %pad_add_fusion.s, bf16[8,2,192,256]{3,2,1,0:T(8,128)(2,1)} %get-tuple-element.66.grads_ref, bf16[1,1,3,2048,3584]{4,3,2,1,0:T(8,128)(2,1)} %w3.5, bf16[1,1,3,2048,3584]{4,3,2,1,0:T(8,128)(2,1)} %w3.5, bf16[1,1,3,2048,3584]{4,3,2,1,0:T(8,128)(2,1)} %w3.5, ...), custom_call_target="tpu_custom_call" | custom-call | flops 2818572288 | bytes 14680064 | tf_op jit(solution)/shard_map/input_other/pallas_call | solution.py:347
  103.4 4.5 %collective-permute-done.9.refs_5_ = bf16[192,1792]{1,0:T(8,128)(2,1)S(1)} collective-permute-done((bf16[192,1792]{1,0:T(8,128)(2,1)S(1)}, bf16[192,1792]{1,0:T(8,128)(2,1)S(1)}, u32[]{:S(2)}, u32[]{:S(2)}) %collective-permute-start.9) | collective-permute-done | bytes 688160 | tf_op jit(solution)/shard_map/ppermute | solution.py:494
  107.9 0.8 slice_bitcast_fusion.3
  108.8 6.5 %collective-permute-done.5.refs_1_ = bf16[2,2,2,192,128]{4,3,2,1,0:T(8,128)(2,1)S(1)} collective-permute-done((bf16[2,2,2,192,128]{4,3,2,1,0:T(8,128)(2,1)}, bf16[2,2,2,192,128]{4,3,2,1,0:T(8,128)(2,1)S(1)}, u32[]{:S(2)}, u32[]{:S(2)}) %collective-permute-start.5) | collective-permute-done | bytes 393248 | tf_op jit(solution)/shard_map/ppermute | solution.py:494
  115.4 0.7 slice_bitcast_fusion.2
  116.6 3.7 %shard_map.115 = (bf16[64,1792]{1,0:T(8,128)(2,1)}, bf16[64,1792]{1,0:T(8,128)(2,1)}, bf16[64,1792]{1,0:T(8,128)(2,1)}, bf16[64,1792]{1,0:T(8,128)(2,1)}) custom-call(s32[1]{0:T(128)} %bitcast.6.s, bf16[2,2,1,192,128]{4,3,2,1,0:T(8,128)(2,1)} %bitcast.41, bf16[2,2,1,192,128]{4,3,2,1,0:T(8,128)(2,1)} %bitcast.43, bf16[2,1,192,128]{3,2,1,0:T(8,128)(2,1)} %bitcast.45, ...), custom_call_target="tpu_custom_call" | custom-call | flops 704643072 | bytes 3670016 | tf_op jit(solution)/shard_map/pallas_call | solution.py:400
  120.4 3.8 %shard_map.116 = (bf16[64,1792]{1,0:T(8,128)(2,1)}, bf16[64,1792]{1,0:T(8,128)(2,1)}, bf16[64,1792]{1,0:T(8,128)(2,1)}, bf16[64,1792]{1,0:T(8,128)(2,1)}) custom-call(s32[1]{0:T(128)} %bitcast.6.s, bf16[2,2,1,192,128]{4,3,2,1,0:T(8,128)(2,1)} %bitcast.42, bf16[2,2,1,192,128]{4,3,2,1,0:T(8,128)(2,1)} %bitcast.44, bf16[2,1,192,128]{3,2,1,0:T(8,128)(2,1)} %bitcast.46, ...), custom_call_target="tpu_custom_call" | custom-call | flops 704643072 | bytes 3670016 | tf_op jit(solution)/shard_map/pallas_call | solution.py:400
  124.2 2.1 collective-permute-start.39
  126.3 3.7 %shard_map.114 = (bf16[64,1792]{1,0:T(8,128)(2,1)}, bf16[64,1792]{1,0:T(8,128)(2,1)}, bf16[64,1792]{1,0:T(8,128)(2,1)}, bf16[64,1792]{1,0:T(8,128)(2,1)}) custom-call(s32[1]{0:T(128)} %bitcast.6.s, bf16[2,2,2,192,128]{4,3,2,1,0:T(8,128)(2,1)} %copy-done, bf16[2,2,2,192,128]{4,3,2,1,0:T(8,128)(2,1)} %copy-done.1, bf16[2,2,192,128]{3,2,1,0:T(8,128)(2,1)} %copy-done.6, ...), custom_call_target="tpu_custom_call" | custom-call | flops 704643072 | bytes 3670016 | tf_op jit(solution)/shard_map/pallas_call | solution.py:400
  130.0 0.7 collective-permute-start.25
  130.7 1.1 add.173
  131.8 3.7 %shard_map.113 = (bf16[64,1792]{1,0:T(8,128)(2,1)}, bf16[64,1792]{1,0:T(8,128)(2,1)}, bf16[64,1792]{1,0:T(8,128)(2,1)}, bf16[64,1792]{1,0:T(8,128)(2,1)}) custom-call(s32[1]{0:T(128)} %bitcast.6.s, bf16[2,2,2,192,128]{4,3,2,1,0:T(8,128)(2,1)} %copy-done, bf16[2,2,2,192,128]{4,3,2,1,0:T(8,128)(2,1)} %copy-done.1, bf16[2,2,192,128]{3,2,1,0:T(8,128)(2,1)} %copy-done.6, ...), custom_call_target="tpu_custom_call" | custom-call | flops 704643072 | bytes 3670016 | tf_op jit(solution)/shard_map/pallas_call | solution.py:400
  135.5 1.5 collective-permute-start.32
  137.2 0.6 copy-done.13
  137.8 3.7 %shard_map.112 = (bf16[64,1792]{1,0:T(8,128)(2,1)}, bf16[64,1792]{1,0:T(8,128)(2,1)}, bf16[64,1792]{1,0:T(8,128)(2,1)}, bf16[64,1792]{1,0:T(8,128)(2,1)}) custom-call(s32[1]{0:T(128)} %bitcast.6.s, bf16[2,2,2,192,128]{4,3,2,1,0:T(8,128)(2,1)} %copy-done, bf16[2,2,2,192,128]{4,3,2,1,0:T(8,128)(2,1)} %copy-done.1, bf16[2,2,192,128]{3,2,1,0:T(8,128)(2,1)} %copy-done.6, ...), custom_call_target="tpu_custom_call" | custom-call | flops 704643072 | bytes 3670016 | tf_op jit(solution)/shard_map/pallas_call | solution.py:400
  141.5 3.8 %shard_map.111 = (bf16[64,1792]{1,0:T(8,128)(2,1)}, bf16[64,1792]{1,0:T(8,128)(2,1)}, bf16[64,1792]{1,0:T(8,128)(2,1)}, bf16[64,1792]{1,0:T(8,128)(2,1)}) custom-call(s32[1]{0:T(128)} %bitcast.6.s, bf16[2,2,2,192,128]{4,3,2,1,0:T(8,128)(2,1)} %copy-done, bf16[2,2,2,192,128]{4,3,2,1,0:T(8,128)(2,1)} %copy-done.1, bf16[2,2,192,128]{3,2,1,0:T(8,128)(2,1)} %copy-done.6, ...), custom_call_target="tpu_custom_call" | custom-call | flops 704643072 | bytes 3670016 | tf_op jit(solution)/shard_map/pallas_call | solution.py:400
  145.3 0.9 collective-permute-start.22
  146.2 1.2 collective-permute-start.16
  147.4 0.8 collective-permute-start.13
  148.4 1.3 collective-permute-start.38
  149.7 2.1 collective-permute-start.40
  151.7 2.1 collective-permute-done.22
  153.8 0.8 collective-permute-start.24
  154.6 4.1 %collective-permute-done.16 = bf16[64,1792]{1,0:T(8,128)(2,1)S(1)} collective-permute-done((bf16[64,1792]{1,0:T(8,128)(2,1)S(1)}, bf16[64,1792]{1,0:T(8,128)(2,1)S(1)}, u32[]{:S(2)}, u32[]{:S(2)}) %collective-permute-start.16) | collective-permute-done | bytes 229408 | tf_op jit(solution)/shard_map/ppermute | solution.py:494
  158.8 0.8 collective-permute-start.21
  159.6 4.2 %collective-permute-done.13 = bf16[64,1792]{1,0:T(8,128)(2,1)} collective-permute-done((bf16[64,1792]{1,0:T(8,128)(2,1)}, bf16[64,1792]{1,0:T(8,128)(2,1)}, u32[]{:S(2)}, u32[]{:S(2)}) %collective-permute-start.13) | collective-permute-done | bytes 229408 | tf_op jit(solution)/shard_map/ppermute | solution.py:494
  163.8 2.1 collective-permute-start.26
  165.9 9.4 %input_own.1 = f32[192,1792]{1,0:T(8,128)} custom-call(s32[48]{0:T(128)} %pad_add_fusion.s, bf16[8,2,192,256]{3,2,1,0:T(8,128)(2,1)} %get-tuple-element.66.grads_ref, bf16[1,1,3,2048,3584]{4,3,2,1,0:T(8,128)(2,1)} %w3.5, bf16[1,1,3,2048,3584]{4,3,2,1,0:T(8,128)(2,1)} %w3.5, bf16[1,1,3,2048,3584]{4,3,2,1,0:T(8,128)(2,1)} %w3.5, bf16[1,1,3,2048,3584]{4,3,2,1,0:T(8,128)(2,1)} %w3.5), custom_call_target="tpu_custom_call" | custom-call | flops 2818572288 | bytes 14680064 | tf_op jit(solution)/shard_map/input_own/pallas_call | solution.py:347
  175.4 1.1 add.168
  176.5 0.7 collective-permute-start.15
  177.2 1.4 collective-permute-start.12
  178.6 2.9 %collective-permute-start.17 = (bf16[64,1792]{1,0:T(8,128)(2,1)S(1)}, bf16[64,1792]{1,0:T(8,128)(2,1)S(1)}, u32[]{:S(2)}, u32[]{:S(2)}) collective-permute-start(bf16[64,1792]{1,0:T(8,128)(2,1)S(1)} %add.169), channel_id=1, source_target_pairs={{0,16},{2,18},{4,20},{6,22},{8,24},{10,26},{12,28},{14,30},{16,0},... | collective-permute-start | bytes 688136 | tf_op jit(solution)/shard_map/ppermute | solution.py:494
  181.6 2.1 add_convert_fusion
  183.7 4.2 %adam.3 = (f32[3,64,3584]{2,1,0:T(8,128)}, f32[3,64,3584]{2,1,0:T(8,128)}, f32[3,64,3584]{2,1,0:T(8,128)}) custom-call(s32[1]{0:T(128)} %bitcast.5.s, bf16[64,1792]{1,0:T(8,128)(2,1)} %get-tuple-element.93.refs_0_, bf16[64,1792]{1,0:T(8,128)(2,1)} %copy-done.18, bf16[64,1792]{1,0:T(8,128)(2,1)} %copy-done.19, bf16[64,1792]{1,0:T(8,128)(2,1)} %get-tuple-element.97.refs_3_, ...), custom_call_target="tpu_custom_call" | custom-call | flops 4587520 | bytes 6422528 | tf_op jit(solution)/shard_map/adam/pallas_call | solution.py:454
  187.9 8.1 %collective-permute-done.23.refs_2_ = bf16[64,1792]{1,0:T(8,128)(2,1)S(1)} collective-permute-done((bf16[64,1792]{1,0:T(8,128)(2,1)S(1)}, bf16[64,1792]{1,0:T(8,128)(2,1)S(1)}, u32[]{:S(2)}, u32[]{:S(2)}) %collective-permute-start.23) | collective-permute-done | bytes 229408 | tf_op jit(solution)/shard_map/ppermute | solution.py:494
  196.0 0.7 copy-done.34
  196.7 3.9 %adam.4 = (f32[3,64,3584]{2,1,0:T(8,128)}, f32[3,64,3584]{2,1,0:T(8,128)}, f32[3,64,3584]{2,1,0:T(8,128)}) custom-call(s32[1]{0:T(128)} %bitcast.5.s, bf16[64,1792]{1,0:T(8,128)(2,1)} %get-tuple-element.83.refs_0_, bf16[64,1792]{1,0:T(8,128)(2,1)} %copy-done.29, ...), custom_call_target="tpu_custom_call", output_to_operand_aliasing={{0}: (10, {}), {1}: (11, {}), {2}: (12, {})} | custom-call | flops 4587520 | bytes 6422528 | tf_op jit(solution)/shard_map/adam/pallas_call | solution.py:454
  200.9 4.8 %collective-permute-done.14.refs_2_ = bf16[64,1792]{1,0:T(8,128)(2,1)S(1)} collective-permute-done((bf16[64,1792]{1,0:T(8,128)(2,1)S(1)}, bf16[64,1792]{1,0:T(8,128)(2,1)S(1)}, u32[]{:S(2)}, u32[]{:S(2)}) %collective-permute-start.14) | collective-permute-done | bytes 229408 | tf_op jit(solution)/shard_map/ppermute | solution.py:494
  205.7 0.7 copy-done.33
  206.4 3.9 %adam.5 = (f32[3,64,3584]{2,1,0:T(8,128)}, f32[3,64,3584]{2,1,0:T(8,128)}, f32[3,64,3584]{2,1,0:T(8,128)}) custom-call(s32[1]{0:T(128)} %bitcast.5.s, bf16[64,1792]{1,0:T(8,128)(2,1)} %get-tuple-element.75.refs_0_, bf16[64,1792]{1,0:T(8,128)(2,1)} %copy-done.30, ...), custom_call_target="tpu_custom_call", output_to_operand_aliasing={{0}: (10, {}), {1}: (11, {}), {2}: (12, {})} | custom-call | flops 4587520 | bytes 6422528 | tf_op jit(solution)/shard_map/adam/pallas_call | solution.py:454
  (130 shorter events, 3.0 us)
Async XLA Ops:
  0.6 53.6 %collective-permute-start.29 = (bf16[192,1792]{1,0:T(8,128)(2,1)}, bf16[192,1792]{1,0:T(8,128)(2,1)}, u32[]{:S(2)}, u32[]{:S(2)}) collective-permute-start(bf16[192,1792]{1,0:T(8,128)(2,1)} %refs_4_.7), channel_id=1, source_target_pairs={{0,8},{2,10},{4,12},{6,14},{8,0},{10,2},{12,4},{14,6},{16,24},{18,... | collective-permute-start | bytes 2064392 | tf_op jit(solution)/shard_map/ppermute | solution.py:494
  3.7 62.3 %collective-permute-start.30 = (bf16[192,1792]{1,0:T(8,128)(2,1)}, bf16[192,1792]{1,0:T(8,128)(2,1)}, u32[]{:S(2)}, u32[]{:S(2)}) collective-permute-start(bf16[192,1792]{1,0:T(8,128)(2,1)} %refs_4_.7), channel_id=1, source_target_pairs={{0,2},{2,0},{4,6},{6,4},{8,10},{10,8},{12,14},{14,12},{16,18},{18,... | collective-permute-start | bytes 2064392 | tf_op jit(solution)/shard_map/ppermute | solution.py:494
  3.8 18.1 %collective-permute-start = (bf16[192,1792]{1,0:T(8,128)(2,1)}, bf16[192,1792]{1,0:T(8,128)(2,1)S(1)}, u32[]{:S(2)}, u32[]{:S(2)}) collective-permute-start(bf16[192,1792]{1,0:T(8,128)(2,1)} %refs_4_.6), channel_id=1, source_target_pairs={{0,1},{1,0},{2,3},{3,2},{4,5},{5,4},{6,7},{7,6},{8,9},{9,8},{10,11... | collective-permute-start | bytes 2064392 | tf_op jit(solution)/shard_map/ppermute | solution.py:490
  21.8 14.3 %copy-start.2 = (bf16[192,1792]{1,0:T(8,128)(2,1)}, bf16[192,1792]{1,0:T(8,128)(2,1)S(1)}, u32[]{:S(2)}) copy-start(bf16[192,1792]{1,0:T(8,128)(2,1)S(1)} %collective-permute-done.other_ref.refs_4_) | copy-start | bytes 2064388
  21.8 25.8 %collective-permute-start.1 = (bf16[192,1792]{1,0:T(8,128)(2,1)}, bf16[192,1792]{1,0:T(8,128)(2,1)S(1)}, u32[]{:S(2)}, u32[]{:S(2)}) collective-permute-start(bf16[192,1792]{1,0:T(8,128)(2,1)} %refs_4_.7), channel_id=1, source_target_pairs={{0,1},{1,0},{2,3},{3,2},{4,5},{5,4},{6,7},{7,6},{8,9},{9,8},{10,11... | collective-permute-start | bytes 2064392 | tf_op jit(solution)/shard_map/ppermute | solution.py:490
  36.1 12.0 %copy-start.4 = (bf16[192,1792]{1,0:T(8,128)(2,1)S(1)}, bf16[192,1792]{1,0:T(8,128)(2,1)}, u32[]{:S(2)}) copy-start(bf16[192,1792]{1,0:T(8,128)(2,1)} %refs_4_.6) | copy-start | bytes 2064388
  47.6 7.1 %copy-start.14 = (bf16[192,1792]{1,0:T(8,128)(2,1)}, bf16[192,1792]{1,0:T(8,128)(2,1)S(1)}, u32[]{:S(2)}) copy-start(bf16[192,1792]{1,0:T(8,128)(2,1)S(1)} %collective-permute-done.1.other_ref.refs_4_) | copy-start | bytes 2064388
  47.6 17.2 %collective-permute-start.3 = (bf16[2,2,2,1,192,128]{5,4,2,1,3,0:T(8,128)(2,1)}, bf16[2,2,2,1,192,128]{5,4,2,1,3,0:T(8,128)(2,1)}, u32[]{:S(2)}, u32[]{:S(2)}) collective-permute-start(bf16[2,2,2,1,192,128]{5,4,2,1,3,0:T(8,128)(2,1)} %bitcast.47), channel_id=1, source_target_pairs={{0,1},{1,0},{2,3},{3,2},{4,5},{5,4},{6,7},{7,6},{8,9},{9,8},{10,11... | collective-permute-start | bytes 1179656 | tf_op jit(solution)/shard_map/ppermute | solution.py:490
  48.1 22.4 %collective-permute-start.18 = (bf16[192,1792]{1,0:T(8,128)(2,1)S(1)}, bf16[192,1792]{1,0:T(8,128)(2,1)S(1)}, u32[]{:S(2)}, u32[]{:S(2)}) collective-permute-start(bf16[192,1792]{1,0:T(8,128)(2,1)S(1)} %copy-done.4), channel_id=1, source_target_pairs={{0,8},{2,10},{4,12},{6,14},{8,0},{10,2},{12,4},{14,6},{16,24},{18,... | collective-permute-start | bytes 2064392 | tf_op jit(solution)/shard_map/ppermute | solution.py:494
  54.2 20.7 %collective-permute-start.19 = (bf16[192,1792]{1,0:T(8,128)(2,1)S(1)}, bf16[192,1792]{1,0:T(8,128)(2,1)S(1)}, u32[]{:S(2)}, u32[]{:S(2)}) collective-permute-start(bf16[192,1792]{1,0:T(8,128)(2,1)S(1)} %copy-done.4), channel_id=1, source_target_pairs={{0,2},{2,0},{4,6},{6,4},{8,10},{10,8},{12,14},{14,12},{16,18},{18,... | collective-permute-start | bytes 2064392 | tf_op jit(solution)/shard_map/ppermute | solution.py:494
  54.2 23.2 %collective-permute-start.31 = (bf16[192,1792]{1,0:T(8,128)(2,1)}, bf16[192,1792]{1,0:T(8,128)(2,1)}, u32[]{:S(2)}, u32[]{:S(2)}) collective-permute-start(bf16[192,1792]{1,0:T(8,128)(2,1)} %collective-permute-done.29.refs_5_), channel_id=1, source_target_pairs={{0,2},{2,0},{4,6},{6,4},{8,10},{10,8},{12,14},{14,12},{16,18},{18,... | collective-permute-start | bytes 2064392 | tf_op jit(solution)/shard_map/ppermute | solution.py:494
  54.7 20.2 %copy-start.3 = (bf16[192,1792]{1,0:T(8,128)(2,1)S(1)}, bf16[192,1792]{1,0:T(8,128)(2,1)}, u32[]{:S(2)}) copy-start(bf16[192,1792]{1,0:T(8,128)(2,1)} %copy-done.2) | copy-start | bytes 2064388
  64.9 19.5 %collective-permute-start.4 = (bf16[2,2,2,2,192,128]{5,4,3,2,1,0:T(8,128)(2,1)}, bf16[2,2,2,2,192,128]{5,4,3,2,1,0:T(8,128)(2,1)S(1)}, u32[]{:S(2)}, u32[]{:S(2)}) collective-permute-start(bf16[2,2,2,2,192,128]{5,4,3,2,1,0:T(8,128)(2,1)} %get-tuple-element.70), channel_id=1, source_target_pairs={{0,1},{1,0},{2,3},{3,2},{4,5},{5,4},{6,7},{7,6},{8,9},{9,8},{10,11... | collective-permute-start | bytes 2359304 | tf_op jit(solution)/shard_map/ppermute | solution.py:490
  66.1 8.5 %collective-permute-start.8 = (bf16[2,2,1,192,128]{4,3,1,2,0:T(8,128)(2,1)S(1)}, bf16[2,2,1,192,128]{4,3,1,2,0:T(8,128)(2,1)S(1)}, u32[]{:S(2)}, u32[]{:S(2)}) collective-permute-start(bf16[2,2,1,192,128]{4,3,1,2,0:T(8,128)(2,1)S(1)} %bitcast_add_fusion.1), channel_id=1, source_target_pairs={{0,8},{2,10},{4,12},{6,14},{8,0},{10,2},{12,4},{14,6},{16,24},{18,... | collective-permute-start | bytes 589832 | tf_op jit(solution)/shard_map/ppermute | solution.py:494
  69.0 15.4 %copy-start.15 = (bf16[2,2,1,192,128]{4,3,1,0,2:T(8,128)(2,1)}, bf16[2,2,1,192,128]{4,3,1,0,2:T(8,128)(2,1)S(1)}, u32[]{:S(2)}) copy-start(bf16[2,2,1,192,128]{4,3,1,0,2:T(8,128)(2,1)S(1)} %bitcast_add_fusion) | copy-start | bytes 589828
  70.5 32.8 %copy-start.8 = (bf16[192,1792]{1,0:T(8,128)(2,1)}, bf16[192,1792]{1,0:T(8,128)(2,1)S(1)}, u32[]{:S(2)}) copy-start(bf16[192,1792]{1,0:T(8,128)(2,1)S(1)} %collective-permute-done.18.refs_5_) | copy-start | bytes 2064388
  70.5 15.8 %collective-permute-start.20 = (bf16[192,1792]{1,0:T(8,128)(2,1)S(1)}, bf16[192,1792]{1,0:T(8,128)(2,1)S(1)}, u32[]{:S(2)}, u32[]{:S(2)}) collective-permute-start(bf16[192,1792]{1,0:T(8,128)(2,1)S(1)} %collective-permute-done.18.refs_5_), channel_id=1, source_target_pairs={{0,2},{2,0},{4,6},{6,4},{8,10},{10,8},{12,14},{14,12},{16,18},{18,... | collective-permute-start | bytes 2064392 | tf_op jit(solution)/shard_map/ppermute | solution.py:494
  74.6 9.8 %copy-start.16 = (bf16[2,2,1,192,128]{4,3,1,2,0:T(8,128)(2,1)}, bf16[2,2,1,192,128]{4,3,1,2,0:T(8,128)(2,1)S(1)}, u32[]{:S(2)}) copy-start(bf16[2,2,1,192,128]{4,3,1,2,0:T(8,128)(2,1)S(1)} %collective-permute-done.8) | copy-start | bytes 589828
  74.6 18.6 %collective-permute-start.35 = (bf16[192,1792]{1,0:T(8,128)(2,1)}, bf16[192,1792]{1,0:T(8,128)(2,1)}, u32[]{:S(2)}, u32[]{:S(2)}) collective-permute-start(bf16[192,1792]{1,0:T(8,128)(2,1)} %copy-done.14), channel_id=1, source_target_pairs={{0,8},{2,10},{4,12},{6,14},{8,0},{10,2},{12,4},{14,6},{16,24},{18,... | collective-permute-start | bytes 2064392 | tf_op jit(solution)/shard_map/ppermute | solution.py:494
  75.0 28.3 %copy-start.9 = (bf16[192,1792]{1,0:T(8,128)(2,1)}, bf16[192,1792]{1,0:T(8,128)(2,1)S(1)}, u32[]{:S(2)}) copy-start(bf16[192,1792]{1,0:T(8,128)(2,1)S(1)} %collective-permute-done.19.refs_6_) | copy-start | bytes 2064388
  75.0 32.9 %collective-permute-start.9 = (bf16[192,1792]{1,0:T(8,128)(2,1)S(1)}, bf16[192,1792]{1,0:T(8,128)(2,1)S(1)}, u32[]{:S(2)}, u32[]{:S(2)}) collective-permute-start(bf16[192,1792]{1,0:T(8,128)(2,1)S(1)} %copy-done.3), channel_id=1, source_target_pairs={{0,8},{2,10},{4,12},{6,14},{8,0},{10,2},{12,4},{14,6},{16,24},{18,... | collective-permute-start | bytes 2064392 | tf_op jit(solution)/shard_map/ppermute | solution.py:494
  77.4 31.2 %collective-permute-start.36 = (bf16[192,1792]{1,0:T(8,128)(2,1)}, bf16[192,1792]{1,0:T(8,128)(2,1)}, u32[]{:S(2)}, u32[]{:S(2)}) collective-permute-start(bf16[192,1792]{1,0:T(8,128)(2,1)} %copy-done.14), channel_id=1, source_target_pairs={{0,2},{2,0},{4,6},{6,4},{8,10},{10,8},{12,14},{14,12},{16,18},{18,... | collective-permute-start | bytes 2064392 | tf_op jit(solution)/shard_map/ppermute | solution.py:494
  84.4 8.9 %collective-permute-start.27 = (bf16[2,1,192,128]{3,2,0,1:T(8,128)(2,1)S(1)}, bf16[2,1,192,128]{3,2,0,1:T(8,128)(2,1)S(1)}, u32[]{:S(2)}, u32[]{:S(2)}) collective-permute-start(bf16[2,1,192,128]{3,2,0,1:T(8,128)(2,1)S(1)} %slice_bitcast_fusion.5), channel_id=1, source_target_pairs={{0,2},{2,0},{4,6},{6,4},{8,10},{10,8},{12,14},{14,12},{16,18},{18,... | collective-permute-start | bytes 294920 | tf_op jit(solution)/shard_map/ppermute | solution.py:494
  86.3 21.6 %copy-start = (bf16[2,2,2,192,128]{4,3,2,1,0:T(8,128)(2,1)}, bf16[2,2,2,192,128]{4,3,2,1,0:T(8,128)(2,1)S(1)}, u32[]{:S(2)}) copy-start(bf16[2,2,2,192,128]{4,3,2,1,0:T(8,128)(2,1)S(1)} %get-tuple-element.113.refs_0_) | copy-start | bytes 1179652
  86.3 6.9 %copy-start.11 = (bf16[192,1792]{1,0:T(8,128)(2,1)}, bf16[192,1792]{1,0:T(8,128)(2,1)S(1)}, u32[]{:S(2)}) copy-start(bf16[192,1792]{1,0:T(8,128)(2,1)S(1)} %collective-permute-done.20.refs_7_) | copy-start | bytes 2064388
  86.3 16.9 %collective-permute-start.28 = (bf16[2,1,192,128]{3,2,1,0:T(8,128)(2,1)}, bf16[2,1,192,128]{3,2,1,0:T(8,128)(2,1)}, u32[]{:S(2)}, u32[]{:S(2)}) collective-permute-start(bf16[2,1,192,128]{3,2,1,0:T(8,128)(2,1)} %slice_bitcast_fusion.4), channel_id=1, source_target_pairs={{0,2},{2,0},{4,6},{6,4},{8,10},{10,8},{12,14},{14,12},{16,18},{18,... | collective-permute-start | bytes 294920 | tf_op jit(solution)/shard_map/ppermute | solution.py:494
  93.3 22.9 %collective-permute-start.37 = (bf16[192,1792]{1,0:T(8,128)(2,1)}, bf16[192,1792]{1,0:T(8,128)(2,1)}, u32[]{:S(2)}, u32[]{:S(2)}) collective-permute-start(bf16[192,1792]{1,0:T(8,128)(2,1)} %collective-permute-done.35.refs_5_), channel_id=1, source_target_pairs={{0,2},{2,0},{4,6},{6,4},{8,10},{10,8},{12,14},{14,12},{16,18},{18,... | collective-permute-start | bytes 2064392 | tf_op jit(solution)/shard_map/ppermute | solution.py:494
  93.9 21.5 %collective-permute-start.5 = (bf16[2,2,2,192,128]{4,3,2,1,0:T(8,128)(2,1)}, bf16[2,2,2,192,128]{4,3,2,1,0:T(8,128)(2,1)S(1)}, u32[]{:S(2)}, u32[]{:S(2)}) collective-permute-start(bf16[2,2,2,192,128]{4,3,2,1,0:T(8,128)(2,1)} %get-tuple-element.112), channel_id=1, source_target_pairs={{0,8},{2,10},{4,12},{6,14},{8,0},{10,2},{12,4},{14,6},{16,24},{18,... | collective-permute-start | bytes 1179656 | tf_op jit(solution)/shard_map/ppermute | solution.py:494
  103.3 32.2 %collective-permute-start.10 = (bf16[192,1792]{1,0:T(8,128)(2,1)S(1)}, bf16[192,1792]{1,0:T(8,128)(2,1)S(1)}, u32[]{:S(2)}, u32[]{:S(2)}) collective-permute-start(bf16[192,1792]{1,0:T(8,128)(2,1)S(1)} %copy-done.3), channel_id=1, source_target_pairs={{0,2},{2,0},{4,6},{6,4},{8,10},{10,8},{12,14},{14,12},{16,18},{18,... | collective-permute-start | bytes 2064392 | tf_op jit(solution)/shard_map/ppermute | solution.py:494
  107.9 16.3 %copy-start.10 = (bf16[192,1792]{1,0:T(8,128)(2,1)}, bf16[192,1792]{1,0:T(8,128)(2,1)S(1)}, u32[]{:S(2)}) copy-start(bf16[192,1792]{1,0:T(8,128)(2,1)S(1)} %collective-permute-done.9.refs_5_) | copy-start | bytes 2064388
  107.9 29.0 %collective-permute-start.11 = (bf16[192,1792]{1,0:T(8,128)(2,1)S(1)}, bf16[192,1792]{1,0:T(8,128)(2,1)S(1)}, u32[]{:S(2)}, u32[]{:S(2)}) collective-permute-start(bf16[192,1792]{1,0:T(8,128)(2,1)S(1)} %collective-permute-done.9.refs_5_), channel_id=1, source_target_pairs={{0,2},{2,0},{4,6},{6,4},{8,10},{10,8},{12,14},{14,12},{16,18},{18,... | collective-permute-start | bytes 2064392 | tf_op jit(solution)/shard_map/ppermute | solution.py:494
  108.7 36.6 %collective-permute-start.2 = (bf16[192,1792]{1,0:T(8,128)(2,1)}, bf16[192,1792]{1,0:T(8,128)(2,1)}, u32[]{:S(2)}, u32[]{:S(2)}) collective-permute-start(bf16[192,1792]{1,0:T(8,128)(2,1)} %input_other.1), channel_id=1, source_target_pairs={{0,1},{1,0},{2,3},{3,2},{4,5},{5,4},{6,7},{7,6},{8,9},{9,8},{10,11... | collective-permute-start | bytes 2064392 | tf_op jit(solution)/shard_map/ppermute | solution.py:490
  115.4 8.8 %copy-start.1 = (bf16[2,2,2,192,128]{4,3,2,1,0:T(8,128)(2,1)}, bf16[2,2,2,192,128]{4,3,2,1,0:T(8,128)(2,1)S(1)}, u32[]{:S(2)}) copy-start(bf16[2,2,2,192,128]{4,3,2,1,0:T(8,128)(2,1)S(1)} %collective-permute-done.5.refs_1_) | copy-start | bytes 1179652
  115.4 4.9 %collective-permute-start.6 = (bf16[2,2,192,128]{3,2,1,0:T(8,128)(2,1)}, bf16[2,2,192,128]{3,2,1,0:T(8,128)(2,1)S(1)}, u32[]{:S(2)}, u32[]{:S(2)}) collective-permute-start(bf16[2,2,192,128]{3,2,1,0:T(8,128)(2,1)} %slice_bitcast_fusion.3), channel_id=1, source_target_pairs={{0,2},{2,0},{4,6},{6,4},{8,10},{10,8},{12,14},{14,12},{16,18},{18,... | collective-permute-start | bytes 589832 | tf_op jit(solution)/shard_map/ppermute | solution.py:494
  116.2 8.1 %collective-permute-start.7 = (bf16[2,2,192,128]{3,2,1,0:T(8,128)(2,1)}, bf16[2,2,192,128]{3,2,1,0:T(8,128)(2,1)S(1)}, u32[]{:S(2)}, u32[]{:S(2)}) collective-permute-start(bf16[2,2,192,128]{3,2,1,0:T(8,128)(2,1)} %slice_bitcast_fusion.2), channel_id=1, source_target_pairs={{0,2},{2,0},{4,6},{6,4},{8,10},{10,8},{12,14},{14,12},{16,18},{18,... | collective-permute-start | bytes 589832 | tf_op jit(solution)/shard_map/ppermute | solution.py:494
  120.3 9.7 %collective-permute-start.33 = (bf16[64,1792]{1,0:T(8,128)(2,1)}, bf16[64,1792]{1,0:T(8,128)(2,1)}, u32[]{:S(2)}, u32[]{:S(2)}) collective-permute-start(bf16[64,1792]{1,0:T(8,128)(2,1)} %get-tuple-element.96), channel_id=1, source_target_pairs={{0,4},{2,6},{4,0},{6,2},{8,12},{10,14},{12,8},{14,10},{16,20},{18,... | collective-permute-start | bytes 688136 | tf_op jit(solution)/shard_map/ppermute | solution.py:494
  124.2 21.9 %collective-permute-start.39 = (bf16[64,1792]{1,0:T(8,128)(2,1)}, bf16[64,1792]{1,0:T(8,128)(2,1)S(1)}, u32[]{:S(2)}, u32[]{:S(2)}) collective-permute-start(bf16[64,1792]{1,0:T(8,128)(2,1)} %get-tuple-element.100), channel_id=1, source_target_pairs={{0,4},{2,6},{4,0},{6,2},{8,12},{10,14},{12,8},{14,10},{16,20},{18,... | collective-permute-start | bytes 688136 | tf_op jit(solution)/shard_map/ppermute | solution.py:494
  130.0 17.4 %collective-permute-start.25 = (bf16[64,1792]{1,0:T(8,128)(2,1)}, bf16[64,1792]{1,0:T(8,128)(2,1)S(1)}, u32[]{:S(2)}, u32[]{:S(2)}) collective-permute-start(bf16[64,1792]{1,0:T(8,128)(2,1)} %get-tuple-element.90), channel_id=1, source_target_pairs={{0,4},{2,6},{4,0},{6,2},{8,12},{10,14},{12,8},{14,10},{16,20},{18,... | collective-permute-start | bytes 688136 | tf_op jit(solution)/shard_map/ppermute | solution.py:494
  135.5 12.9 %collective-permute-start.32 = (bf16[64,1792]{1,0:T(8,128)(2,1)}, bf16[64,1792]{1,0:T(8,128)(2,1)S(1)}, u32[]{:S(2)}, u32[]{:S(2)}) collective-permute-start(bf16[64,1792]{1,0:T(8,128)(2,1)} %get-tuple-element.94), channel_id=1, source_target_pairs={{0,4},{2,6},{4,0},{6,2},{8,12},{10,14},{12,8},{14,10},{16,20},{18,... | collective-permute-start | bytes 688136 | tf_op jit(solution)/shard_map/ppermute | solution.py:494
  136.9 12.7 %collective-permute-start.34 = (bf16[64,1792]{1,0:T(8,128)(2,1)S(1)}, bf16[64,1792]{1,0:T(8,128)(2,1)S(1)}, u32[]{:S(2)}, u32[]{:S(2)}) collective-permute-start(bf16[64,1792]{1,0:T(8,128)(2,1)S(1)} %add.173), channel_id=1, source_target_pairs={{0,16},{2,18},{4,20},{6,22},{8,24},{10,26},{12,28},{14,30},{16,0},... | collective-permute-start | bytes 688136 | tf_op jit(solution)/shard_map/ppermute | solution.py:494
  141.5 6.7 %copy-start.21 = (bf16[64,1792]{1,0:T(8,128)(2,1)S(1)}, bf16[64,1792]{1,0:T(8,128)(2,1)}, u32[]{:S(2)}) copy-start(bf16[64,1792]{1,0:T(8,128)(2,1)} %get-tuple-element.99) | copy-start | bytes 688132
  141.5 6.7 %copy-start.26 = (bf16[64,1792]{1,0:T(8,128)(2,1)S(1)}, bf16[64,1792]{1,0:T(8,128)(2,1)}, u32[]{:S(2)}) copy-start(bf16[64,1792]{1,0:T(8,128)(2,1)} %get-tuple-element.89) | copy-start | bytes 688132
  145.3 8.5 %collective-permute-start.22 = (bf16[64,1792]{1,0:T(8,128)(2,1)S(1)}, bf16[64,1792]{1,0:T(8,128)(2,1)S(1)}, u32[]{:S(2)}, u32[]{:S(2)}) collective-permute-start(bf16[64,1792]{1,0:T(8,128)(2,1)S(1)} %copy-done.35), channel_id=1, source_target_pairs={{0,4},{2,6},{4,0},{6,2},{8,12},{10,14},{12,8},{14,10},{16,20},{18,... | collective-permute-start | bytes 688136 | tf_op jit(solution)/shard_map/ppermute | solution.py:494
  146.2 12.6 %collective-permute-start.16 = (bf16[64,1792]{1,0:T(8,128)(2,1)S(1)}, bf16[64,1792]{1,0:T(8,128)(2,1)S(1)}, u32[]{:S(2)}, u32[]{:S(2)}) collective-permute-start(bf16[64,1792]{1,0:T(8,128)(2,1)S(1)} %copy-done.36), channel_id=1, source_target_pairs={{0,4},{2,6},{4,0},{6,2},{8,12},{10,14},{12,8},{14,10},{16,20},{18,... | collective-permute-start | bytes 688136 | tf_op jit(solution)/shard_map/ppermute | solution.py:494
  147.4 16.4 %collective-permute-start.13 = (bf16[64,1792]{1,0:T(8,128)(2,1)}, bf16[64,1792]{1,0:T(8,128)(2,1)}, u32[]{:S(2)}, u32[]{:S(2)}) collective-permute-start(bf16[64,1792]{1,0:T(8,128)(2,1)} %get-tuple-element.78), channel_id=1, source_target_pairs={{0,4},{2,6},{4,0},{6,2},{8,12},{10,14},{12,8},{14,10},{16,20},{18,... | collective-permute-start | bytes 688136 | tf_op jit(solution)/shard_map/ppermute | solution.py:494
  148.3 26.9 %copy-start.18 = (bf16[64,1792]{1,0:T(8,128)(2,1)}, bf16[64,1792]{1,0:T(8,128)(2,1)S(1)}, u32[]{:S(2)}) copy-start(bf16[64,1792]{1,0:T(8,128)(2,1)S(1)} %collective-permute-done.32.refs_1_) | copy-start | bytes 688132
  148.4 28.1 %collective-permute-start.38 = (bf16[64,1792]{1,0:T(8,128)(2,1)}, bf16[64,1792]{1,0:T(8,128)(2,1)S(1)}, u32[]{:S(2)}, u32[]{:S(2)}) collective-permute-start(bf16[64,1792]{1,0:T(8,128)(2,1)} %get-tuple-element.98), channel_id=1, source_target_pairs={{0,4},{2,6},{4,0},{6,2},{8,12},{10,14},{12,8},{14,10},{16,20},{18,... | collective-permute-start | bytes 688136 | tf_op jit(solution)/shard_map/ppermute | solution.py:494
  149.7 25.6 %copy-start.19 = (bf16[64,1792]{1,0:T(8,128)(2,1)}, bf16[64,1792]{1,0:T(8,128)(2,1)S(1)}, u32[]{:S(2)}) copy-start(bf16[64,1792]{1,0:T(8,128)(2,1)S(1)} %collective-permute-done.34.refs_2_) | copy-start | bytes 688132
  149.7 27.5 %collective-permute-start.40 = (bf16[64,1792]{1,0:T(8,128)(2,1)S(1)}, bf16[64,1792]{1,0:T(8,128)(2,1)S(1)}, u32[]{:S(2)}, u32[]{:S(2)}) collective-permute-start(bf16[64,1792]{1,0:T(8,128)(2,1)S(1)} %add.174), channel_id=1, source_target_pairs={{0,16},{2,18},{4,20},{6,22},{8,24},{10,26},{12,28},{14,30},{16,0},... | collective-permute-start | bytes 688136 | tf_op jit(solution)/shard_map/ppermute | solution.py:494
  153.8 24.8 %collective-permute-start.24 = (bf16[64,1792]{1,0:T(8,128)(2,1)}, bf16[64,1792]{1,0:T(8,128)(2,1)S(1)}, u32[]{:S(2)}, u32[]{:S(2)}) collective-permute-start(bf16[64,1792]{1,0:T(8,128)(2,1)} %get-tuple-element.88), channel_id=1, source_target_pairs={{0,4},{2,6},{4,0},{6,2},{8,12},{10,14},{12,8},{14,10},{16,20},{18,... | collective-permute-start | bytes 688136 | tf_op jit(solution)/shard_map/ppermute | solution.py:494
  158.8 16.5 %copy-start.20 = (bf16[64,1792]{1,0:T(8,128)(2,1)S(1)}, bf16[64,1792]{1,0:T(8,128)(2,1)}, u32[]{:S(2)}) copy-start(bf16[64,1792]{1,0:T(8,128)(2,1)} %get-tuple-element.85) | copy-start | bytes 688132
  158.8 16.6 %copy-start.23 = (bf16[64,1792]{1,0:T(8,128)(2,1)S(1)}, bf16[64,1792]{1,0:T(8,128)(2,1)}, u32[]{:S(2)}) copy-start(bf16[64,1792]{1,0:T(8,128)(2,1)} %get-tuple-element.81) | copy-start | bytes 688132
  158.8 16.6 %copy-start.24 = (bf16[64,1792]{1,0:T(8,128)(2,1)S(1)}, bf16[64,1792]{1,0:T(8,128)(2,1)}, u32[]{:S(2)}) copy-start(bf16[64,1792]{1,0:T(8,128)(2,1)} %get-tuple-element.77) | copy-start | bytes 688132
  158.8 19.8 %collective-permute-start.21 = (bf16[64,1792]{1,0:T(8,128)(2,1)}, bf16[64,1792]{1,0:T(8,128)(2,1)S(1)}, u32[]{:S(2)}, u32[]{:S(2)}) collective-permute-start(bf16[64,1792]{1,0:T(8,128)(2,1)} %get-tuple-element.84), channel_id=1, source_target_pairs={{0,4},{2,6},{4,0},{6,2},{8,12},{10,14},{12,8},{14,10},{16,20},{18,... | collective-permute-start | bytes 688136 | tf_op jit(solution)/shard_map/ppermute | solution.py:494
  163.8 17.8 %collective-permute-start.26 = (bf16[64,1792]{1,0:T(8,128)(2,1)S(1)}, bf16[64,1792]{1,0:T(8,128)(2,1)S(1)}, u32[]{:S(2)}, u32[]{:S(2)}) collective-permute-start(bf16[64,1792]{1,0:T(8,128)(2,1)S(1)} %add.171), channel_id=1, source_target_pairs={{0,16},{2,18},{4,20},{6,22},{8,24},{10,26},{12,28},{14,30},{16,0},... | collective-permute-start | bytes 688136 | tf_op jit(solution)/shard_map/ppermute | solution.py:494
  176.5 7.2 %copy-start.22 = (bf16[64,1792]{1,0:T(8,128)(2,1)}, bf16[64,1792]{1,0:T(8,128)(2,1)S(1)}, u32[]{:S(2)}) copy-start(bf16[64,1792]{1,0:T(8,128)(2,1)S(1)} %collective-permute-done.38.refs_4_) | copy-start | bytes 688132
  176.5 24.1 %collective-permute-start.15 = (bf16[64,1792]{1,0:T(8,128)(2,1)}, bf16[64,1792]{1,0:T(8,128)(2,1)S(1)}, u32[]{:S(2)}, u32[]{:S(2)}) collective-permute-start(bf16[64,1792]{1,0:T(8,128)(2,1)} %get-tuple-element.80), channel_id=1, source_target_pairs={{0,4},{2,6},{4,0},{6,2},{8,12},{10,14},{12,8},{14,10},{16,20},{18,... | collective-permute-start | bytes 688136 | tf_op jit(solution)/shard_map/ppermute | solution.py:494
  177.2 6.5 %copy-start.25 = (bf16[64,1792]{1,0:T(8,128)(2,1)}, bf16[64,1792]{1,0:T(8,128)(2,1)S(1)}, u32[]{:S(2)}) copy-start(bf16[64,1792]{1,0:T(8,128)(2,1)S(1)} %collective-permute-done.40.refs_5_) | copy-start | bytes 688132
  177.2 23.5 %collective-permute-start.12 = (bf16[64,1792]{1,0:T(8,128)(2,1)}, bf16[64,1792]{1,0:T(8,128)(2,1)S(1)}, u32[]{:S(2)}, u32[]{:S(2)}) collective-permute-start(bf16[64,1792]{1,0:T(8,128)(2,1)} %get-tuple-element.76), channel_id=1, source_target_pairs={{0,4},{2,6},{4,0},{6,2},{8,12},{10,14},{12,8},{14,10},{16,20},{18,... | collective-permute-start | bytes 688136 | tf_op jit(solution)/shard_map/ppermute | solution.py:494
  178.6 9.3 %copy-start.27 = (bf16[64,1792]{1,0:T(8,128)(2,1)}, bf16[64,1792]{1,0:T(8,128)(2,1)S(1)}, u32[]{:S(2)}) copy-start(bf16[64,1792]{1,0:T(8,128)(2,1)S(1)} %collective-permute-done.24.refs_4_) | copy-start | bytes 688132
  178.6 17.4 %collective-permute-start.23 = (bf16[64,1792]{1,0:T(8,128)(2,1)S(1)}, bf16[64,1792]{1,0:T(8,128)(2,1)S(1)}, u32[]{:S(2)}, u32[]{:S(2)}) collective-permute-start(bf16[64,1792]{1,0:T(8,128)(2,1)S(1)} %add.170), channel_id=1, source_target_pairs={{0,16},{2,18},{4,20},{6,22},{8,24},{10,26},{12,28},{14,30},{16,0},... | collective-permute-start | bytes 688136 | tf_op jit(solution)/shard_map/ppermute | solution.py:494
  178.6 9.3 %copy-start.29 = (bf16[64,1792]{1,0:T(8,128)(2,1)}, bf16[64,1792]{1,0:T(8,128)(2,1)S(1)}, u32[]{:S(2)}) copy-start(bf16[64,1792]{1,0:T(8,128)(2,1)S(1)} %collective-permute-done.21.refs_1_) | copy-start | bytes 688132
  178.6 22.3 %collective-permute-start.17 = (bf16[64,1792]{1,0:T(8,128)(2,1)S(1)}, bf16[64,1792]{1,0:T(8,128)(2,1)S(1)}, u32[]{:S(2)}, u32[]{:S(2)}) collective-permute-start(bf16[64,1792]{1,0:T(8,128)(2,1)S(1)} %add.169), channel_id=1, source_target_pairs={{0,16},{2,18},{4,20},{6,22},{8,24},{10,26},{12,28},{14,30},{16,0},... | collective-permute-start | bytes 688136 | tf_op jit(solution)/shard_map/ppermute | solution.py:494
  181.5 24.2 %collective-permute-start.14 = (bf16[64,1792]{1,0:T(8,128)(2,1)S(1)}, bf16[64,1792]{1,0:T(8,128)(2,1)S(1)}, u32[]{:S(2)}, u32[]{:S(2)}) collective-permute-start(bf16[64,1792]{1,0:T(8,128)(2,1)S(1)} %add.168), channel_id=1, source_target_pairs={{0,16},{2,18},{4,20},{6,22},{8,24},{10,26},{12,28},{14,30},{16,0},... | collective-permute-start | bytes 688136 | tf_op jit(solution)/shard_map/ppermute | solution.py:494
  (14 other events, 48.9 us)
